TPU v7x, 128 devices: a whole 4x4x4 slice. The times are simulated.
128 devices in a mesh: section: 2 (over core), vocab: 64 (over x, z, y).
Axes of the slice: x: 4, y: 4, z: 4, core: 2. Of those that a mesh axis runs over, the one named last changes fastest.
Arguments:
- hidden_in: bfloat16 [2, 256, 7168], P(None, ('section', 'vocab')), may hold values from -6 to 6
- gain_ffn: float32 [7168], replicated, may hold values from 0.4 to 1.6
- w_gate: bfloat16 [7168, 18432], P(None, ('section', 'vocab')), may hold values from -0.0625 to 0.0625
- w_up: bfloat16 [7168, 18432], P(None, ('section', 'vocab')), may hold values from -0.0625 to 0.0625
- w_down: bfloat16 [18432, 7168], P(('section', 'vocab')), may hold values from -0.046875 to 0.046875
- gain_final: float32 [7168], replicated, may hold values from 0.4 to 1.6
- head_weight: bfloat16 [7168, 129280], P(None, ('section', 'vocab')), may hold values from -4.5 to 4.5
- sampled_ids: int32 [2, 256], replicated, may hold values from 0 to 129279
- seq_ids: int32 [2, 256], P(None, ('section', 'vocab')), may hold values from 0 to 7, never falling along the last dimension, each value on 1 to 128 neighbouring positions
Outputs:
- token_logprob: float32 [2, 256], P(None, ('section', 'vocab'))
- log_norm: float32 [2, 256], P(None, ('section', 'vocab'))
- top_mass: float32 [2, 256], P(None, ('section', 'vocab'))
- seq_logprob: float32 [2, 8], replicated
All inputs are finite; a program needn't handle non-finite values.
Results may differ from a plain program's by a relative error of at most 0.006.
Values may be sent and summed in bfloat16 or wider, within the bound.
A program may use at most 192 MiB of HBM per device.

v0:
```python
import jax
import jax.numpy as jnp
from jax import lax
from jax.sharding import Mesh
from jax.sharding import PartitionSpec as P

SEQS = 8
TOPK = 20
SECTION_VOCAB = ("section", "vocab_0", "vocab_1", "vocab_2")


epsilon = 1e-06


def collected_together(shard, axis):
    leaves = jax.tree.leaves(shard)
    sequence = sorted(range(len(leaves)), key=lambda k: -leaves[k].size)
    width = (1, *leaves[sequence[0]].shape)[-1]
    lines = [
        jnp.pad(leaves[k].reshape(-1), (0, -leaves[k].size % width)).reshape(-1, width)
        for k in sequence
    ]
    both, at, found = (lax.all_gather(jnp.concatenate(lines), axis), 0, {})
    for k, line in zip(sequence, lines):
        slab = both[:, at : at + len(line)].reshape(len(both), -1)
        found[k] = slab[:, : leaves[k].size].reshape(-1, *leaves[k].shape)
        at += len(line)
    numbers = iter(range(len(leaves)))
    return jax.tree.map(lambda _: found[next(numbers)], shard)


def combined_by_axis(shard, axes, combine):
    for axis in axes:
        pieces = collected_together(shard, axis)
        shard = jax.tree.map(lambda part: part[0], pieces)
        for k in range(1, lax.axis_size(axis)):
            shard = combine(shard, jax.tree.map(lambda part: part[k], pieces))
    return shard


def over_axes(shard, axes):
    for axis in axes:
        shard = lax.psum(shard, axis)
    return shard


def rms_norm(values, scale_gain):
    wide = values.astype(jnp.float32)
    square_mean = jnp.mean(wide * wide, axis=-1, keepdims=True)
    return (wide * lax.rsqrt(square_mean + epsilon) * scale_gain).astype(jnp.bfloat16)


def largest(values):
    return lax.sort(values, dimension=values.ndim - 1)[..., -TOPK:]


def finish(peak_value, sum_total, sampled_logit, leaders_all):
    log_norm = peak_value + jnp.log(sum_total)
    top_mass = jnp.sum(jnp.exp(leaders_all - log_norm[:, None]), axis=1)
    return (sampled_logit - log_norm, log_norm, top_mass)


def join_stats(left_stats, right_stats):
    peak_value = jnp.maximum(left_stats[0], right_stats[0])
    sum_total = left_stats[1] * jnp.exp(left_stats[0] - peak_value) + right_stats[1] * jnp.exp(
        right_stats[0] - peak_value
    )
    sampled_logit = left_stats[2] + right_stats[2]
    leaders_all = largest(jnp.concatenate([left_stats[3], right_stats[3]], axis=1))
    return (peak_value, sum_total, sampled_logit, leaders_all)


def body(hidden_in, gain_ffn, w_gate, w_up, w_down, gain_final, head_weight, sampled_ids, seq_ids):
    row_count = hidden_in.shape[1]
    shard_width = head_weight.shape[1]
    position = lax.axis_index(SECTION_VOCAB)
    first_row = position * row_count
    columns = lax.broadcasted_iota(jnp.int32, (1, shard_width), 1) + position * shard_width
    logprob_list = []
    norm_list = []
    mass_list = []
    partials = []
    for microbatch in range(hidden_in.shape[0]):
        own_rows = hidden_in[microbatch]
        gathered = lax.all_gather(own_rows, SECTION_VOCAB, axis=0, tiled=True)
        normed = rms_norm(gathered, gain_ffn)
        gate_proj = jnp.dot(normed, w_gate, preferred_element_type=jnp.float32)
        up_proj = jnp.dot(normed, w_up, preferred_element_type=jnp.float32)
        hidden_act = (jax.nn.silu(gate_proj) * up_proj).astype(jnp.bfloat16)
        branch = lax.psum(
            jnp.dot(hidden_act, w_down, preferred_element_type=jnp.float32), SECTION_VOCAB
        )
        residual = (gathered.astype(jnp.float32) + branch).astype(jnp.bfloat16)
        scaled = rms_norm(residual, gain_final)
        logits = jnp.dot(scaled, head_weight, preferred_element_type=jnp.float32)
        token_ids = sampled_ids[microbatch]
        matches = columns == token_ids[:, None]
        sampled_part = jnp.sum(jnp.where(matches, logits, 0.0), axis=1)
        leaders = largest(logits)
        local_peak = jnp.max(logits, axis=1)
        local_total = jnp.sum(jnp.exp(logits - local_peak[:, None]), axis=1)
        merged = combined_by_axis(
            (local_peak, local_total, sampled_part, leaders), SECTION_VOCAB, join_stats
        )
        results = finish(merged[0], merged[1], merged[2], merged[3])
        token_logprob, log_norm, top_mass = [
            lax.dynamic_slice_in_dim(value, first_row, row_count, 0) for value in results
        ]
        onehot = (
            seq_ids[microbatch][:, None] == jnp.arange(SEQS, dtype=jnp.int32)[None, :]
        ).astype(jnp.float32)
        partials.append(jnp.sum(token_logprob[:, None] * onehot, axis=0))
        logprob_list.append(token_logprob)
        norm_list.append(log_norm)
        mass_list.append(top_mass)
    seq_logprob = over_axes(jnp.stack(partials), SECTION_VOCAB)
    return (jnp.stack(logprob_list), jnp.stack(norm_list), jnp.stack(mass_list), seq_logprob)


def solution(mesh):
    split = Mesh(
        mesh.devices.reshape(mesh.shape["section"], 4, 4, 4),
        ("section", "vocab_0", "vocab_1", "vocab_2"),
    )
    return jax.shard_map(
        body,
        mesh=split,
        in_specs=(
            P(None, SECTION_VOCAB, None),
            P(),
            P(None, SECTION_VOCAB),
            P(None, SECTION_VOCAB),
            P(SECTION_VOCAB, None),
            P(),
            P(None, SECTION_VOCAB),
            P(),
            P(None, SECTION_VOCAB),
        ),
        out_specs=(P(None, SECTION_VOCAB), P(None, SECTION_VOCAB), P(None, SECTION_VOCAB), P()),
        check_vma=False,
    )
```

profile of v0, /device:TPU:0, one launch (start us, length us, event | category | flops | bytes accessed | tf_op | source)
XLA Modules:
  0.0 669.0 jit_solution(9942431343124560244)
XLA Ops:
  9.7 73.0 %all-gather.21.cloned.1.call-done = bf16[1,256,7168]{2,0,1:T(2,128)(2,1)} async-done(((bf16[1,2,7168]{2,0,1:T(2,128)(2,1)}), bf16[1,256,7168]{2,0,1:T(2,128)(2,1)}) %all-gather.21.cloned.1.call-update) | async-done | bytes 3670032 | tf_op jit(solution)/shard_map/all_gather | solution.py:85
  82.6 6.6 fusion.6
  89.2 63.0 %all-gather.23.cloned.1.call-done = bf16[1,256,7168]{2,0,1:T(2,128)(2,1)} async-done(((bf16[1,2,7168]{2,0,1:T(2,128)(2,1)}), bf16[1,256,7168]{2,0,1:T(2,128)(2,1)}) %all-gather.23.cloned.1.call-update) | async-done | bytes 3670032 | tf_op jit(solution)/shard_map/all_gather | solution.py:85
  152.2 4.9 fusion.10
  160.4 9.9 %fusion.25 = f32[256,7168]{1,0:T(8,128)} fusion(bf16[144,7168]{1,0:T(8,128)(2,1)S(1)} %copy-done, bf16[7168,144]{0,1:T(8,128)(2,1)} %param.12, bf16[1,256,7168]{2,1,0:T(8,128)(2,1)} %get-tuple-element.105, f32[7168]{0:T(1024)S(1)} %copy-done.8, f32[256]{0:T(256)S(1)} %add_rsqrt_fusion.3, f32[256,144]{0,1:T(8,128)S(1)} %fusion.32), kind=kOutput, calls=%fused_computation.35 | convolution fusion | flops 1064525824 | bytes 15315968 | tf_op jit(solution)/shard_map/dot_general | solution.py:91
  170.4 10.1 %fusion.24 = f32[256,7168]{1,0:T(8,128)} fusion(bf16[144,7168]{1,0:T(8,128)(2,1)S(1)} %copy-done, bf16[7168,144]{0,1:T(8,128)(2,1)} %param.12, bf16[1,256,7168]{2,1,0:T(8,128)(2,1)} %copy-done.4, f32[256]{0:T(256)S(1)} %add_rsqrt_fusion.1, f32[7168]{0:T(1024)S(1)} %copy-done.8, f32[256,144]{0,1:T(8,128)S(1)} %fusion.28), kind=kOutput, calls=%fused_computation.34 | convolution fusion | flops 1064525824 | bytes 15315968 | tf_op jit(solution)/shard_map/dot_general | solution.py:91
  181.2 171.1 %all-reduce.27.cloned.1.call-done = (f32[256,7168]{1,0:T(8,128)}, f32[256,7168]{1,0:T(8,128)}) async-done(((f32[256,7168]{1,0:T(8,128)}, f32[256,7168]{1,0:T(8,128)}), (f32[256,7168]{1,0:T(8,128)}, f32[256,7168]{1,0:T(8,128)})) %all-reduce.27.cloned.1.call-update) | async-done | bytes 14680080 | tf_op jit(solution)/shard_map/psum | solution.py:90
  352.3 8.5 %fusion = (f32[256]{0:T(256)S(1)}, f32[256]{0:T(256)S(1)}) fusion(f32[256,7168]{1,0:T(8,128)} %get-tuple-element.79, bf16[1,256,7168]{2,1,0:T(8,128)(2,1)} %get-tuple-element.105, f32[256,7168]{1,0:T(8,128)} %get-tuple-element.78, bf16[1,256,7168]{2,1,0:T(8,128)(2,1)} %copy-done.4), kind=kLoop, calls=%fused_computation.10 | loop fusion | flops 22019584 | bytes 22022144 | tf_op jit(solution)/shard_map/reduce_sum | solution.py:49
  360.9 10.4 %fusion.97 = (f32[256]{0:T(256)S(1)}, f32[256,1010]{0,1:T(8,128)S(1)}) fusion(bf16[7168,1010]{0,1:T(8,128)(2,1)} %param.15, f32[256]{0:T(256)S(1)} %add_rsqrt_fusion, f32[7168]{0:T(1024)S(1)} %copy-done.12, f32[256,7168]{1,0:T(8,128)} %get-tuple-element.78, bf16[1,256,7168]{2,1,0:T(8,128)(2,1)S(1)} %copy-done.5), kind=kOutput, calls=%fused_computation.212 | convolution fusion | flops 3719819520 | bytes 26554368 | tf_op jit(solution)/shard_map/dot_general | solution.py:95
  371.3 8.9 %fusion.96 = (f32[256]{0:T(256)S(1)}, f32[256,1010]{0,1:T(8,128)S(1)}) fusion(bf16[7168,1010]{0,1:T(8,128)(2,1)} %param.15, f32[7168]{0:T(1024)S(1)} %copy-done.12, f32[256]{0:T(256)S(1)} %add_rsqrt_fusion.2, f32[256,7168]{1,0:T(8,128)S(1)} %bitcast.195, bf16[1,256,7168]{2,1,0:T(8,128)(2,1)S(1)} %copy-done.3), kind=kOutput, calls=%fused_computation.211 | convolution fusion | flops 3719819520 | bytes 26554368 | tf_op jit(solution)/shard_map/dot_general | solution.py:95
  381.7 59.0 %sort.308 = (f32[256,1010]{0,1:T(8,128)}, s32[256,1010]{0,1:T(8,128)}) sort(f32[256,1010]{0,1:T(8,128)} %copy-done.7, s32[256,1010]{0,1:T(8,128)S(1)} %iota.77.clone), dimensions={1}, to_apply=%region_3.4 | sort | flops 4654080 | bytes 4136960 | tf_op jit(solution)/shard_map/sort | solution.py:54
  442.7 1.9 all-gather.10
  447.7 12.0 %all-gather.11 = f32[4,295,20]{1,2,0:T(8,128)S(1)} all-gather(f32[1,295,20]{1,2,0:T(8,128)S(1)} %maximum_bitcast_fusion.1), channel_id=4, replica_groups=mesh['section'=2,'vocab_0'=4,'vocab_1'=4,'vocab_2'=4] {'vocab_0'}, dimensions={0}, use_global_device_ids=true | all-gather | bytes 118000 | tf_op jit(solution)/shard_map/all_gather | solution.py:23
  466.7 12.0 %all-gather.12 = f32[4,295,20]{1,2,0:T(8,128)S(1)} all-gather(f32[1,295,20]{1,2,0:T(8,128)S(1)} %maximum_bitcast_fusion.2), channel_id=5, replica_groups=mesh['section'=2,'vocab_0'=4,'vocab_1'=4,'vocab_2'=4] {'vocab_1'}, dimensions={0}, use_global_device_ids=true | all-gather | bytes 118000 | tf_op jit(solution)/shard_map/all_gather | solution.py:23
  478.8 58.9 %sort.316 = (f32[256,1010]{0,1:T(8,128)}, s32[256,1010]{0,1:T(8,128)}) sort(f32[256,1010]{0,1:T(8,128)} %copy-done.6, s32[256,1010]{0,1:T(8,128)S(1)} %iota.77.clone), dimensions={1}, to_apply=%region_17.18 | sort | flops 4654080 | bytes 4136960 | tf_op jit(solution)/shard_map/sort | solution.py:54
  540.2 1.9 all-gather.14
  542.1 1.8 sort.317
  545.2 12.2 %all-gather.15 = f32[4,295,20]{1,2,0:T(8,128)S(1)} all-gather(f32[1,295,20]{1,2,0:T(8,128)S(1)} %maximum_bitcast_fusion.5), channel_id=9, replica_groups=mesh['section'=2,'vocab_0'=4,'vocab_1'=4,'vocab_2'=4] {'vocab_0'}, dimensions={0}, use_global_device_ids=true | all-gather | bytes 118000 | tf_op jit(solution)/shard_map/all_gather | solution.py:23
  557.6 1.8 sort.318
  559.4 1.8 sort.319
  561.2 1.8 sort.320
  564.4 12.0 %all-gather.16 = f32[4,295,20]{1,2,0:T(8,128)S(1)} all-gather(f32[1,295,20]{1,2,0:T(8,128)S(1)} %maximum_bitcast_fusion.6), channel_id=10, replica_groups=mesh['section'=2,'vocab_0'=4,'vocab_1'=4,'vocab_2'=4] {'vocab_1'}, dimensions={0}, use_global_device_ids=true | all-gather | bytes 118000 | tf_op jit(solution)/shard_map/all_gather | solution.py:23
  576.5 1.8 sort.313
  578.4 1.8 sort.314
  583.4 12.3 %all-gather.13 = f32[4,295,20]{1,2,0:T(8,128)S(1)} all-gather(f32[1,295,20]{1,2,0:T(8,128)S(1)} %maximum_bitcast_fusion.3), channel_id=6, replica_groups=mesh['section'=2,'vocab_0'=4,'vocab_1'=4,'vocab_2'=4] {'vocab_2'}, dimensions={0}, use_global_device_ids=true | all-gather | bytes 118000 | tf_op jit(solution)/shard_map/all_gather | solution.py:23
  595.8 1.8 sort.321
  597.6 1.8 sort.322
  602.6 12.0 %all-gather.17 = f32[4,295,20]{1,2,0:T(8,128)S(1)} all-gather(f32[1,295,20]{1,2,0:T(8,128)S(1)} %maximum_bitcast_fusion.7), channel_id=11, replica_groups=mesh['section'=2,'vocab_0'=4,'vocab_1'=4,'vocab_2'=4] {'vocab_2'}, dimensions={0}, use_global_device_ids=true | all-gather | bytes 118000 | tf_op jit(solution)/shard_map/all_gather | solution.py:23
  616.6 2.5 psum.44
  619.0 9.6 %psum.45 = f32[2,8]{1,0:T(2,128)S(1)} all-reduce(f32[2,8]{1,0:T(2,128)S(1)} %psum.44), channel_id=1, replica_groups=mesh['section'=2,'vocab_0'=4,'vocab_1'=4,'vocab_2'=4] {'vocab_0'}, use_global_device_ids=true, to_apply=%region_39.40 | all-reduce | flops 16 | bytes 128 | tf_op jit(solution)/shard_map/psum | solution.py:43
  628.6 10.1 %psum.46 = f32[2,8]{1,0:T(2,128)S(1)} all-reduce(f32[2,8]{1,0:T(2,128)S(1)} %psum.45), channel_id=1, replica_groups=mesh['section'=2,'vocab_0'=4,'vocab_1'=4,'vocab_2'=4] {'vocab_1'}, use_global_device_ids=true, to_apply=%region_40.41 | all-reduce | flops 16 | bytes 128 | tf_op jit(solution)/shard_map/psum | solution.py:43
  638.7 10.2 %psum.47 = f32[2,8]{1,0:T(2,128)} all-reduce(f32[2,8]{1,0:T(2,128)S(1)} %psum.46), channel_id=1, replica_groups=mesh['section'=2,'vocab_0'=4,'vocab_1'=4,'vocab_2'=4] {'vocab_2'}, use_global_device_ids=true, to_apply=%region_41.42 | all-reduce | flops 16 | bytes 128 | tf_op jit(solution)/shard_map/psum | solution.py:43
  (323 shorter events, 46.4 us)
Async XLA Ops:
  7.2 153.3 %copy-start = (bf16[144,7168]{1,0:T(8,128)(2,1)S(1)}, bf16[144,7168]{1,0:T(8,128)(2,1)}, u32[]{:S(2)}) copy-start(bf16[144,7168]{1,0:T(8,128)(2,1)} %param.13) | copy-start | bytes 6193156
  7.2 75.4 %all-gather.21.cloned.1.call-start = ((), (), s32[]{:S(2)}) async-start(), calls=%async_computation | async-start | bytes 7397376 | tf_op jit(solution)/shard_map/all_gather | solution.py:85
  8.9 143.3 %all-gather.23.cloned.1.call-start = ((), (), s32[]{:S(2)}) async-start(), calls=%async_computation.1 | async-start | bytes 7397376 | tf_op jit(solution)/shard_map/all_gather | solution.py:85
  9.6 342.7 %all-reduce.27.cloned.1.call-start = ((), (), s32[]{:S(2)}) async-start(), calls=%async_computation.2 | async-start | bytes 29360128 | tf_op jit(solution)/shard_map/psum | solution.py:90
  89.2 68.0 %copy-start.8 = (f32[7168]{0:T(1024)S(1)}, f32[7168]{0:T(1024)}, u32[]{:S(2)}) copy-start(f32[7168]{0:T(1024)} %param.10) | copy-start | bytes 86020
  152.2 5.0 copy-start.2
  152.2 5.0 copy-start.11
  157.1 1.8 copy-start.4
  180.5 0.7 copy-start.10
  180.5 0.7 copy-start.9
  352.3 8.5 %copy-start.5 = (bf16[1,256,7168]{2,1,0:T(8,128)(2,1)S(1)}, bf16[1,256,7168]{2,1,0:T(8,128)(2,1)}, u32[]{:S(2)}) copy-start(bf16[1,256,7168]{2,1,0:T(8,128)(2,1)} %copy-done.4) | copy-start | bytes 11010052
  352.3 8.5 %copy-start.12 = (f32[7168]{0:T(1024)S(1)}, f32[7168]{0:T(1024)}, u32[]{:S(2)}) copy-start(f32[7168]{0:T(1024)} %param.14) | copy-start | bytes 86020
  352.3 18.9 %slice-start = ((s8[7340032]{0:T(1024)(128)(4,1)}), s8[4194304]{0:T(1024)(128)(4,1)S(1)}, s32[]{:S(2)}) async-start(s8[7340032]{0:T(1024)(128)(4,1)} %bitcast.194), calls=%async_computation.3 | async-start | bytes 8388608
  360.8 10.4 %copy-start.3 = (bf16[1,256,7168]{2,1,0:T(8,128)(2,1)S(1)}, bf16[1,256,7168]{2,1,0:T(8,128)(2,1)}, u32[]{:S(2)}) copy-start(bf16[1,256,7168]{2,1,0:T(8,128)(2,1)} %get-tuple-element.105) | copy-start | bytes 11010052
  360.8 10.4 %slice-start.1 = ((s8[7340032]{0:T(1024)(128)(4,1)}), s8[3145728]{0:T(1024)(128)(4,1)S(1)}, s32[]{:S(2)}) async-start(s8[7340032]{0:T(1024)(128)(4,1)} %bitcast.194), calls=%async_computation.4 | async-start | bytes 6291456
  371.3 8.9 %copy-start.6 = (f32[256,1010]{0,1:T(8,128)}, f32[256,1010]{0,1:T(8,128)S(1)}, u32[]{:S(2)}) copy-start(f32[256,1010]{0,1:T(8,128)S(1)} %get-tuple-element.227) | copy-start | bytes 3102724
  380.2 1.0 copy-start.7
  478.7 183.3 %copy-start.1 = (bf16[144,7168]{1,0:T(8,128)(2,1)S(1)}, bf16[144,7168]{1,0:T(8,128)(2,1)}, u32[]{:S(2)}) copy-start(bf16[144,7168]{1,0:T(8,128)(2,1)} %param.13) | copy-start | bytes 6193156
Sparse Core Ops, SparseCore 0:
  11.1 71.4 all-gather.20
  85.8 66.3 all-gather.22
  180.6 171.5 all-reduce.26
where the time goes:
time: 678 us; the launch traced here: 669 us
  waiting for transfers between devices  307 us (45%)
  other arithmetic  178 us (26%)
  blocking collectives  109 us (16%)
  matrix products  42.3 us (6%)
  local copies, waits for them, and re-layouts  18 us (3%)
  between operations  15.2 us (2%)
    psum x1, waiting for transfers between devices, body(): lax.psum(jnp.dot(hidden_act, w_down, preferred_element_type=jnp.float32),...  171 us
    sort x22, other arithmetic, largest(): return lax.sort(values, dimension=values.ndim - 1)[..., -TOPK:]  154 us
    all_gather x2, waiting for transfers between devices, body(): gathered = lax.all_gather(own_rows, SECTION_VOCAB, axis=0, tiled=True)  136 us
    all_gather x8, blocking collectives, collected_together(): both, at, found = (lax.all_gather(jnp.concatenate(lines), axis), 0, {})  76.4 us
    psum x4, blocking collectives, over_axes(): shard = lax.psum(shard, axis)  32.3 us
    dot_general x2, matrix products, body(): jnp.dot(hidden_act, w_down, preferred_element_type=jnp.float32)  20.1 us
    reduce_sum x3, other arithmetic, rms_norm(): square_mean = jnp.mean(wide * wide, axis=-1, keepdims=True)  20 us
    dot_general x2, matrix products, body(): logits = jnp.dot(scaled, head_weight, preferred_element_type=jnp.float32)  19.3 us
  transfers between devices with their start and end apart: 3, of which 3 were waited for; matrix products, arithmetic and copies ran while one was open for 1% of the time, Pallas kernels for 0%

commit v1 on v0

v1 whole, which is shorter than its diff:
```python
import functools

import jax
import jax.numpy as jnp
from jax import lax
from jax.experimental import pallas as pl
from jax.experimental.pallas import tpu as pltpu
from jax.sharding import Mesh
from jax.sharding import PartitionSpec as P

SEQS = 8
TOPK = 20
EPS = 1e-06
NEG = -3.0e38
MESH = pl.DeviceIdType.MESH
CORE = "section"
AXES = ("x", "z", "y")
EVERY = (CORE,) + AXES
ORDERS = ((0, 1, 2), (1, 2, 0), (2, 0, 1))
N = 4


def pick(sel):
    return tuple(sel.get(i, slice(None)) for i in range(3))


def column_groups(width):
    tiles = width // 128
    cuts = [0, (tiles + 2) // 3, (2 * tiles + 2) // 3, tiles]
    return [pl.ds(128 * cuts[q], 128 * (cuts[q + 1] - cuts[q])) for q in range(3)]


def toward(axis, k):
    name = AXES[axis]
    return {name: lax.rem(lax.axis_index(name) + k, N)}


def partner():
    return {CORE: 1 - lax.axis_index(CORE)}


def meet():
    barrier = pltpu.get_barrier_semaphore()
    for axis in range(3):
        for k in (1, 2, 3):
            pl.semaphore_signal(barrier, inc=1, device_id=toward(axis, k), device_id_type=MESH)
    pl.semaphore_signal(barrier, inc=1, device_id=partner(), device_id_type=MESH)
    pl.semaphore_wait(barrier, 10)


class Mail:
    def __init__(self, send_sem, recv_sem):
        self.send_sem, self.recv_sem = send_sem, recv_sem
        self.copies, self.count = {}, 0

    def send(self, tag, src, dst, device):
        copy = pltpu.make_async_remote_copy(
            src_ref=src,
            dst_ref=dst,
            send_sem=self.send_sem.at[self.count],
            recv_sem=self.recv_sem.at[self.count],
            device_id=device,
            device_id_type=MESH,
        )
        copy.start()
        self.count += 1
        self.copies.setdefault(tag, []).append(copy)

    def received(self, tag):
        for copy in self.copies[tag]:
            copy.wait_recv()

    def all_sent(self):
        for copies in self.copies.values():
            for copy in copies:
                copy.wait_send()


def gather_start(buf, mail, groups):
    def go(q, tag, sel, axis):
        for k in (1, 3, 2):
            src, dst = dict(sel), dict(sel)
            src[axis], dst[axis] = 0, N - k
            rest = (slice(None), groups[q])
            mail.send((q, tag), buf.at[pick(src) + rest], buf.at[pick(dst) + rest], toward(axis, k))

    others = pl.ds(1, 3)
    for q, (a, b, c) in enumerate(ORDERS):
        go(q, "a", {b: 0, c: 0}, a)
    for q, (a, b, c) in enumerate(ORDERS):
        go(q, "b0", {a: 0, c: 0}, b)
    for q, (a, b, c) in enumerate(ORDERS):
        go(q, "c0", {a: 0, b: 0}, c)
    for q, (a, b, c) in enumerate(ORDERS):
        mail.received((q, "a"))
        go(q, "b1", {a: others, c: 0}, b)
    for q, (a, b, c) in enumerate(ORDERS):
        go(q, "c1", {a: others, b: 0}, c)
    for q, (a, b, c) in enumerate(ORDERS):
        mail.received((q, "b0"))
        go(q, "c2", {a: 0, b: others}, c)
    for q, (a, b, c) in enumerate(ORDERS):
        mail.received((q, "b1"))
        go(q, "c3", {a: others, b: others}, c)
    for tag in ("c0", "c1", "c2", "c3"):
        for q in range(3):
            mail.received((q, tag))


def settle(buf, out):
    @pl.loop(0, N)
    def _(i):
        @pl.loop(0, N)
        def _(j):
            for k in range(N):
                out[i * N + j, pl.ds(4 * k, 4), :] = buf[i, j, k]


def rms(wide, gain):
    mean = jnp.mean(wide * wide, axis=-1, keepdims=True)
    return (wide * lax.rsqrt(mean + EPS) * gain).astype(jnp.bfloat16)


def block_kernel(
    h_ref, gf_ref, gl_ref, wg_ref, wu_ref, wd_ref, hw_ref,
    x2_ref, hw2_ref,
    G, G2, X, S, R1, R2, R3, T1, T2, F, PB, W, WD, ACT,
    own_sem, swap_s, swap_r, g_s, g_r, r_s, r_r, g2_s, g2_r,
):
    groups = column_groups(h_ref.shape[-1])
    width = h_ref.shape[-1]
    loads = []
    for n, (src, dst) in enumerate(((wg_ref, W.at[0]), (wu_ref, W.at[1]), (wd_ref, WD.at[0]))):
        copy = pltpu.make_async_copy(src, dst, own_sem.at[n])
        copy.start()
        loads.append(copy)
    meet()
    G[0, 0, 0] = rms(h_ref[...].astype(jnp.float32), gf_ref[...])
    swap = Mail(swap_s, swap_r)
    for tag, src, dst in (("g", wg_ref, W.at[2]), ("u", wu_ref, W.at[3]), ("d", wd_ref, WD.at[1])):
        swap.send(tag, src, dst, partner())
    mail = Mail(g_s, g_r)
    gather_start(G, mail, groups)
    settle(G, X)
    for copy in loads:
        copy.wait()
    for tag in ("g", "u", "d"):
        swap.received(tag)
    swap.send("h", hw_ref, hw2_ref, partner())

    rows = N * N * N * 4
    hidden = W.shape[1]
    y = lax.dot_general(
        W[...].reshape(4 * hidden, width), X[...].reshape(rows, width), (((1,), (1,)), ((), ())),
        preferred_element_type=jnp.float32,
    )
    acts = []
    for p in range(2):
        gate, up = y[2 * p * hidden : (2 * p + 1) * hidden], y[(2 * p + 1) * hidden : (2 * p + 2) * hidden]
        acts.append(gate / (1.0 + jnp.exp(-gate)) * up)
    ACT[...] = jnp.concatenate(acts, axis=0).T.astype(jnp.bfloat16)
    step = PB.shape[-1]

    @pl.loop(0, width // step)
    def _(n):
        cols = pl.ds(pl.multiple_of(n * step, 128), step)
        down = WD[:, :, cols].reshape(2 * hidden, step)
        part = jnp.dot(ACT[...], down, preferred_element_type=jnp.float32)
        PB[...] = part.astype(jnp.bfloat16).reshape(PB.shape)
        for i in range(N):
            for j in range(N):
                for k in range(N):
                    S[i, j, k, :, cols] = PB[i * N + j, pl.ds(4 * k, 4), :]

    red = Mail(r_s, r_r)
    for k in (1, 3, 2):
        for q, (a, b, c) in enumerate(ORDERS):
            rest = (slice(None), groups[q])
            red.send((q, 1), S.at[pick({c: k}) + rest], R1.at[(k - 1, slice(None), slice(None)) + rest], toward(c, k))
    for q, (a, b, c) in enumerate(ORDERS):
        cols = groups[q]
        red.received((q, 1))

        @pl.loop(0, N)
        def _(i):
            @pl.loop(0, N)
            def _(j):
                left = [i, j]
                sel = {ax: left.pop(0) for ax in range(3) if ax != c}
                sel[c] = 0
                total = S[pick(sel) + (slice(None), cols)].astype(jnp.float32)
                for k in range(3):
                    total += R1[k, i, j, :, cols].astype(jnp.float32)
                T1[i, j, :, cols] = total.astype(jnp.bfloat16)

        first = min(a, b)
        for k in (1, 3, 2):
            src = T1.at[k, :, :, cols] if b == first else T1.at[:, k, :, cols]
            red.send((q, 2), src, R2.at[k - 1, :, :, cols], toward(b, k))
    for q, (a, b, c) in enumerate(ORDERS):
        cols = groups[q]
        red.received((q, 2))
        first = min(a, b)
        for i in range(N):
            total = (T1[0, i, :, cols] if b == first else T1[i, 0, :, cols]).astype(jnp.float32)
            for k in range(3):
                total += R2[k, i, :, cols].astype(jnp.float32)
            T2[i, :, cols] = total.astype(jnp.bfloat16)
        for k in (1, 3, 2):
            red.send((q, 3), T2.at[k, :, cols], R3.at[k - 1, :, cols], toward(a, k))
    for q in range(3):
        cols = groups[q]
        red.received((q, 3))
        total = T2[0, :, cols].astype(jnp.float32)
        for k in range(3):
            total += R3[k, :, cols].astype(jnp.float32)
        F[:, cols] = total

    residual = (h_ref[...].astype(jnp.float32) + F[...]).astype(jnp.bfloat16)
    G2[0, 0, 0] = rms(residual.astype(jnp.float32), gl_ref[...])
    mail2 = Mail(g2_s, g2_r)
    gather_start(G2, mail2, groups)
    settle(G2, x2_ref)
    swap.received("h")
    for m in (mail, swap, red, mail2):
        m.all_sent()


def dense_block(h, gain_ffn, gain_final, w_gate, w_up, w_down, head):
    hidden, width = w_gate.shape
    bf16, f32 = jnp.bfloat16, jnp.float32
    vmem, anywhere = pl.BlockSpec(memory_space=pltpu.VMEM), pl.BlockSpec(memory_space=pl.ANY)
    dma = lambda n: pltpu.SemaphoreType.DMA((n,))
    return pl.pallas_call(
        block_kernel,
        out_shape=(
            jax.ShapeDtypeStruct((N * N, N * 4, width), bf16),
            jax.ShapeDtypeStruct(head.shape, bf16),
        ),
        in_specs=[vmem, vmem, vmem, anywhere, anywhere, anywhere, anywhere],
        out_specs=(vmem, anywhere),
        scratch_shapes=[
            pltpu.VMEM((N, N, N, 4, width), bf16),
            pltpu.VMEM((N, N, N, 4, width), bf16),
            pltpu.VMEM((N * N, N * 4, width), bf16),
            pltpu.VMEM((N, N, N, 4, width), bf16),
            pltpu.VMEM((3, N, N, 4, width), bf16),
            pltpu.VMEM((3, N, 4, width), bf16),
            pltpu.VMEM((3, 4, width), bf16),
            pltpu.VMEM((N, N, 4, width), bf16),
            pltpu.VMEM((N, 4, width), bf16),
            pltpu.VMEM((4, width), f32),
            pltpu.VMEM((N * N, N * 4, 512), bf16),
            pltpu.VMEM((4, hidden, width), bf16),
            pltpu.VMEM((2, hidden, width), bf16),
            pltpu.VMEM((N**3 * 4, 2 * hidden), bf16),
            dma(3), dma(4), dma(4), dma(63), dma(63), dma(27), dma(27), dma(63), dma(63),
        ],
        compiler_params=pltpu.CompilerParams(collective_id=0, has_side_effects=True, vmem_limit_bytes=62 << 20),
        name="dense_block",
    )(h, gain_ffn, gain_final, w_gate, w_up, w_down, head)


def sort_pairs(n):
    pairs, p = [], 1
    while p < n:
        k = p
        while k >= 1:
            for j in range(k % p, n - k, 2 * k):
                for i in range(min(k, n - j - k)):
                    if (i + j) // (2 * p) == (i + j + k) // (2 * p):
                        pairs.append((i + j, i + j + k))
            k //= 2
        p *= 2
    return pairs


def sort_down(values):
    values = list(values)
    for i, j in sort_pairs(len(values)):
        values[i], values[j] = jnp.maximum(values[i], values[j]), jnp.minimum(values[i], values[j])
    return values


def merge_down(left, right, keep=TOPK):
    left = list(left) + [False] * (keep - len(left))
    right = list(right) + [False] * (keep - len(right))

    def order(u, v):
        if u is None or v is False:
            return u, v
        if v is None or u is False:
            return v, u
        return jnp.maximum(u, v), jnp.minimum(u, v)

    line = [order(left[i], right[keep - 1 - i])[0] for i in range(keep)] + [None] * (32 - keep)
    gap = 16
    while gap:
        for i in range(32):
            if not i & gap:
                line[i], line[i + gap] = order(line[i], line[i + gap])
        gap //= 2
    return line[32 - keep :]


def head_kernel(x_ref, ids_ref, own_ref, other_ref, st_ref, LT, M, Q, V, *, columns):
    step = pl.program_id(0)
    rows, width = x_ref.shape[0] * x_ref.shape[1], x_ref.shape[2]
    wide = own_ref.shape[0]
    half = pl.num_programs(0) // 2

    def logits_of(w_ref):
        x = x_ref[...].reshape(rows, width)
        logits = lax.dot_general(
            w_ref[...], x, (((1,), (1,)), ((), ())), preferred_element_type=jnp.float32
        )
        place = lax.broadcasted_iota(jnp.int32, (wide, rows), 0) + lax.rem(step, half) * wide
        LT[pl.ds(pl.multiple_of(step * wide, wide), wide), :] = jnp.where(place < columns, logits, NEG)

    @pl.when(step < half)
    def _():
        logits_of(own_ref)

    @pl.when(step >= half)
    def _():
        logits_of(other_ref)

    @pl.when(step == pl.num_programs(0) - 1)
    def _():
        levels, lane_tiles = 16, rows // 128
        deep = LT.shape[0] // levels
        place = lax.axis_index(CORE), [lax.axis_index(n) for n in AXES]
        chip = (place[1][0] * N + place[1][1]) * N + place[1][2]
        first = (place[0] * N**3 + chip) * columns
        second = ((1 - place[0]) * N**3 + chip) * columns
        for t in range(lane_tiles):
            lanes = pl.ds(128 * t, 128)
            ids = ids_ref[:, lanes]

            @pl.loop(0, deep // 16)
            def _(j):
                both = []
                for side in range(2):
                    at = pl.multiple_of(side * (deep // 2) + j * 8, 8)
                    both.append(sort_down([LT[pl.ds(l * deep + at, 8), lanes] for l in range(levels)]))
                for l, value in enumerate(merge_down(*both)):
                    M[l, pl.ds(pl.multiple_of(j * 8, 8), 8), lanes] = value

            have = deep // 16
            while have > 1:
                have //= 2

                @pl.loop(0, have)
                def _(j):
                    both = []
                    for side in range(2):
                        at = pl.multiple_of((side * have + j) * 8, 8)
                        both.append([M[l, pl.ds(at, 8), lanes] for l in range(TOPK)])
                    for l, value in enumerate(merge_down(*both)):
                        M[l, pl.ds(pl.multiple_of(j * 8, 8), 8), lanes] = value

            top = [M[l, pl.ds(0, 8), lanes] for l in range(TOPK)]
            for shift in (4, 2, 1):
                top = merge_down(top, [pltpu.roll(v, shift, 0) for v in top])
            peak = top[0]

            def body(j, carry):
                total, hit = carry
                at = pl.multiple_of(j * 8, 8)
                value = LT[pl.ds(at, 8), lanes]
                row = lax.broadcasted_iota(jnp.int32, (8, 128), 0) + at
                late = row >= LT.shape[0] // 2
                column = jnp.where(late, row - LT.shape[0] // 2, row)
                token = column + jnp.where(late, second, first)
                same = (token == ids) & (column < columns)
                return total + jnp.exp(value - peak), hit + jnp.where(same, value, 0.0)

            zero = jnp.zeros((8, 128), jnp.float32)
            total, hit = lax.fori_loop(0, LT.shape[0] // 8, body, (zero, zero), unroll=8)
            for l in range(TOPK):
                Q[pl.ds(l, 1), lanes] = top[l][0:1]
            Q[pl.ds(TOPK, 1), lanes] = jnp.sum(total, axis=0, keepdims=True)
            Q[pl.ds(TOPK + 1, 1), lanes] = jnp.sum(hit, axis=0, keepdims=True)
            Q[pl.ds(TOPK + 2, 2), lanes] = jnp.zeros((2, 128), jnp.float32)
            Q[pl.ds(24, 104), lanes] = jnp.zeros((104, 128), jnp.float32)
        V[...] = Q[...].T
        for i in range(N):
            for j in range(N):
                for k in range(N):
                    st_ref[i, j, k] = V[pl.ds(((i * N + j) * N + k) * 4, 4), :]


def head_stats(x, ids, own, other):
    columns, width = own.shape
    wide = 256
    half = -(-columns // wide)
    rows = x.shape[0] * x.shape[1]
    f32 = jnp.float32
    return pl.pallas_call(
        functools.partial(head_kernel, columns=columns),
        out_shape=jax.ShapeDtypeStruct((N, N, N, 4, 128), f32),
        grid=(2 * half,),
        in_specs=[
            pl.BlockSpec(x.shape, lambda s: (0, 0, 0), pipeline_mode=pl.Buffered(1)),
            pl.BlockSpec(ids.shape, lambda s: (0, 0)),
            pl.BlockSpec((wide, width), lambda s: (jnp.minimum(s, half - 1), 0)),
            pl.BlockSpec((wide, width), lambda s: (jnp.maximum(s - half, 0), 0)),
        ],
        out_specs=pl.BlockSpec((N, N, N, 4, 128), lambda s: (0, 0, 0, 0, 0)),
        scratch_shapes=[
            pltpu.VMEM((2 * half * wide, rows), f32),
            pltpu.VMEM((TOPK, half * wide // 16, rows), f32),
            pltpu.VMEM((128, rows), f32),
            pltpu.VMEM((rows, 128), f32),
        ],
        compiler_params=pltpu.CompilerParams(dimension_semantics=("arbitrary",), vmem_limit_bytes=60 << 20),
        name="head_stats",
    )(x, ids, own, other)


def finish_kernel(st_ref, sid_ref, lp_ref, ln_ref, tm_ref, sq_ref, U1, U2, U3, B, Q, A, a_s, a_r, q_s, q_r):
    meet()
    mail = Mail(a_s, a_r)
    for k in (1, 3, 2):
        mail.send(1, st_ref.at[:, :, k], U1.at[N - k], toward(2, k))
    U1[0] = st_ref[:, :, 0]
    mail.received(1)
    for k in (1, 3, 2):
        mail.send(2, U1.at[:, :, k], U2.at[N - k], toward(1, k))
    U2[0] = U1[:, :, 0]
    mail.received(2)
    for k in (1, 3, 2):
        mail.send(3, U2.at[:, :, k], U3.at[N - k], toward(0, k))
    U3[0] = U2[:, :, 0]
    mail.received(3)
    for i in range(N):
        for j in range(N):
            for k in range(N):
                B[pl.ds(((i * N + j) * N + k) * 4, 4), :] = U3[i, j, k]
    Q[...] = B[...].T

    def line(l):
        return [Q[pl.ds(l, 1), pl.ds(128 * t, 128)] for t in range(2)]

    lists = [line(l) for l in range(TOPK)]
    top = merge_down([v[0] for v in lists], [v[1] for v in lists])
    for shift in (64, 32, 16, 8, 4):
        top = merge_down(top, [pltpu.roll(v, shift, 1) for v in top])
    peak = top[0]
    sums, hits = line(TOPK), line(TOPK + 1)
    total = sum(s * jnp.exp(v - peak) for s, v in zip(sums, lists[0]))
    hit = hits[0] + hits[1]
    for shift in (64, 32, 16, 8, 4):
        total = total + pltpu.roll(total, shift, 1)
        hit = hit + pltpu.roll(hit, shift, 1)
    log_norm = peak + jnp.log(total)
    mass = sum(jnp.exp(v - log_norm) for v in top)
    logprob = hit - log_norm
    for ref, value in ((lp_ref, logprob), (ln_ref, log_norm), (tm_ref, mass)):
        ref[0:1, :] = value[:, 0:2]
        ref[1:2, :] = pltpu.roll(value, 126, 1)[:, 0:2]

    lane = lax.broadcasted_iota(jnp.int32, (1, 128), 1)
    turned = [logprob] + [pltpu.roll(logprob, j, 1) for j in (1, 2, 3)]
    part = jnp.zeros((1, 128), jnp.float32)
    for t in range(4):
        spread = turned[0]
        for j in (1, 2, 3):
            spread = jnp.where(lax.rem(lane - t + 4, 4) == j, turned[j], spread)
        mine = (lane // SEQS == t // 2) & (lax.rem(lane, SEQS) == sid_ref[t // 2, t % 2])
        part = part + jnp.where(mine, spread, 0.0)
    A[0, 0] = jnp.broadcast_to(part, (8, 128))
    seq = Mail(q_s, q_r)
    seq.send(0, A.at[0, 0], A.at[0, 1], partner())
    seq.received(0)
    both = A[0, 0] + A[0, 1]
    for axis in range(3):
        A[axis + 1, 0] = both
        for k in (1, 3, 2):
            seq.send(axis + 1, A.at[axis + 1, 0], A.at[axis + 1, N - k], toward(axis, k))
        seq.received(axis + 1)
        got = [A[axis + 1, k] for k in range(N)]
        both = (got[0] + got[2]) + (got[1] + got[3])
    sq_ref[0:1, :] = both[0:1, 0:SEQS]
    sq_ref[1:2, :] = pltpu.roll(both, 128 - SEQS, 1)[0:1, 0:SEQS]
    mail.all_sent()
    seq.all_sent()


def finish(stats, seq_ids):
    f32 = jnp.float32
    vmem = pl.BlockSpec(memory_space=pltpu.VMEM)
    dma = lambda n: pltpu.SemaphoreType.DMA((n,))
    small = jax.ShapeDtypeStruct(seq_ids.shape, f32)
    tile = (4, 128)
    return pl.pallas_call(
        finish_kernel,
        out_shape=(small, small, small, jax.ShapeDtypeStruct((2, SEQS), f32)),
        in_specs=[vmem, pl.BlockSpec(memory_space=pltpu.SMEM)],
        out_specs=(vmem, vmem, vmem, vmem),
        scratch_shapes=[
            pltpu.VMEM((N, N, N) + tile, f32),
            pltpu.VMEM((N, N, N) + tile, f32),
            pltpu.VMEM((N, N, N) + tile, f32),
            pltpu.VMEM((N**3 * 4, 128), f32),
            pltpu.VMEM((128, N**3 * 4), f32),
            pltpu.VMEM((4, N, 8, 128), f32),
            dma(9), dma(9), dma(10), dma(10),
        ],
        compiler_params=pltpu.CompilerParams(collective_id=1, has_side_effects=True),
        name="finish",
    )(stats, seq_ids)


def body(hidden_in, gain_ffn, w_gate, w_up, w_down, gain_final, head_weight, sampled_ids, seq_ids):
    batches, own, width = hidden_in.shape
    place = jnp.arange(N**3 * 4, dtype=jnp.int32)
    chip = jnp.int32(0)
    for n, name in enumerate(AXES):
        offset = place // (4 * N ** (2 - n)) % N
        chip = chip * N + (lax.axis_index(name) + offset) % N
    device = lax.axis_index(CORE) * N**3 + chip
    slot = (place % 4) // own * sampled_ids.shape[1] + device * own + place % own
    flat = sampled_ids.reshape(-1)
    ids = jnp.sum(jnp.where(slot[None, :] == jnp.arange(flat.size)[:, None], flat[:, None], 0), axis=0)

    head = head_weight.T
    x, other_head = dense_block(
        hidden_in.reshape(batches * own, width), gain_ffn.reshape(1, width), gain_final.reshape(1, width),
        w_gate.T, w_up.T, w_down, head,
    )
    stats = head_stats(x, ids.reshape(1, -1), head, other_head)
    return tuple(finish(stats, seq_ids))


def solution(mesh):
    split = Mesh(mesh.devices.reshape(mesh.shape["section"], N, N, N), EVERY)
    rows = P(None, EVERY)
    return jax.shard_map(
        body,
        mesh=split,
        in_specs=(P(None, EVERY, None), P(), rows, rows, P(EVERY, None), P(), rows, P(), rows),
        out_specs=(rows, rows, rows, P()),
        check_vma=False,
    )
```

time: 678 us -> 141 us (0.21); the launches traced: 669 us -> 141 us
  waiting for transfers between devices: 307 us -> 0 us
  other arithmetic: 178 us -> 0.74 us
  Pallas kernels: 0 us -> 132 us
  blocking collectives: 109 us -> 0 us
  matrix products: 42.3 us -> 0 us
  between operations: 15.2 us -> 0.66 us
  local copies, waits for them, and re-layouts: 18 us -> 7.05 us
    psum x1 -> x0, waiting for transfers between devices: 171 us -> none  [body(): lax.psum(jnp.dot(hidden_act, w_down, preferred_element_type=jnp.float32),...]
    sort x22 -> x0, other arithmetic: 154 us -> none  [largest(): return lax.sort(values, dimension=values.ndim - 1)[..., -TOPK:]]
    all_gather x2 -> x0, waiting for transfers between devices: 136 us -> none  [body(): gathered = lax.all_gather(own_rows, SECTION_VOCAB, axis=0, tiled=True)]
    pallas_call x0 -> x3, Pallas kernels: none -> 132 us  [the longest x1 84.9 us: dense_block(): pl.pallas_call(block_kernel, out_shape=(jax.ShapeDtypeStruct((N * N, N *...]
    all_gather x8 -> x0, blocking collectives: 76.4 us -> none  [collected_together(): both, at, found = (lax.all_gather(jnp.concatenate(lines), axis), 0, {})]
    dot_general x6 -> x0, matrix products: 42.3 us -> none  [the longest x2 20.1 us: body(): jnp.dot(hidden_act, w_down, preferred_element_type=jnp.float32)]
    psum x4 -> x0, blocking collectives: 32.3 us -> none  [over_axes(): shard = lax.psum(shard, axis)]
    reduce_sum x8 -> x1, other arithmetic: 20.8 us -> 0.71 us  [body(): jnp.sum(jnp.where(slot[None, :] == jnp.arange(flat.size)[:, None], flat[:...]
  transfers between devices with their start and end apart: 3 -> 0, of which waited for: 3 -> 0; matrix products, arithmetic and copies ran while one was open for 1% -> 0% of each run, Pallas kernels for 0% -> 0%
where the time goes in v1:
time: 141 us
  Pallas kernels  132 us (94%)
  local copies, waits for them, and re-layouts  7.05 us (5%)
    pallas_call x1, Pallas kernels, dense_block(): pl.pallas_call(block_kernel, out_shape=(jax.ShapeDtypeStruct((N * N, N *...  84.9 us
    pallas_call x1, Pallas kernels, finish(): pl.pallas_call(finish_kernel, out_shape=(small, small, small, jax.ShapeDt...  26.9 us
    pallas_call x1, Pallas kernels, head_stats(): pl.pallas_call(functools.partial(head_kernel, columns=columns), out_shape...  20.4 us
    unnamed x5, local copies, waits for them, and re-layouts  5.59 us

profile of v1, /device:TPU:0, one launch (start us, length us, event | category | flops | bytes accessed | tf_op | source)
XLA Modules:
  0.0 140.7 jit_solution(2153237476222272687)
XLA Ops:
  0.7 0.7 copy.13
  1.3 0.7 select_reduce_fusion
  2.1 1.5 %reshape.157.h_ref = bf16[4,7168]{1,0:T(4,128)(2,1)} reshape(bf16[2,2,7168]{2,1,0:T(2,128)(2,1)} %param.9) | data formatting | bytes 114688 | tf_op jit(solution)/shard_map/reshape | solution.py:529
  3.5 84.9 %dense_block.1 = (bf16[16,16,7168]{2,1,0:T(8,128)(2,1)}, bf16[1010,7168]{1,0:T(8,128)(2,1)}) custom-call(bf16[4,7168]{1,0:T(4,128)(2,1)} %reshape.157.h_ref, f32[1,7168]{1,0:T(1,128)} %bitcast.12, f32[1,7168]{1,0:T(1,128)} %bitcast.13, bf16[144,7168]{1,0:T(8,128)(2,1)} %bitcast.10, bf16[144,7168]{1,0:T(8,128)(2,1)} %bitcast.11, bf16[144,7168]{1,0:T(8,128)(2,1)} %wd_ref.1, ...), custom_call_target="tpu_custom_call" | custom-call | tf_op jit(solution)/shard_map/dense_block/pallas_call | solution.py:234
  88.4 20.4 %head_stats.1.st_ref = f32[4,4,4,4,128]{4,3,2,1,0:T(4,128)} custom-call(bf16[16,16,7168]{2,1,0:T(8,128)(2,1)} %get-tuple-element.6.x_ref, s32[1,256]{1,0:T(1,128)} %bitcast.15, bf16[1010,7168]{1,0:T(8,128)(2,1)} %bitcast.9, bf16[1010,7168]{1,0:T(8,128)(2,1)} %get-tuple-element.7.other_ref), custom_call_target="tpu_custom_call" | custom-call | tf_op jit(solution)/shard_map/head_stats/pallas_call | solution.py:399
  108.8 26.9 %finish.1 = (f32[2,2]{1,0:T(2,128)}, f32[2,2]{1,0:T(2,128)}, f32[2,2]{1,0:T(2,128)}, f32[2,8]{1,0:T(2,128)}) custom-call(f32[4,4,4,4,128]{4,3,2,1,0:T(4,128)} %head_stats.1.st_ref, s32[2,2]{1,0:T(2,128)} %sid_ref.1), custom_call_target="tpu_custom_call" | custom-call | tf_op jit(solution)/shard_map/finish/pallas_call | solution.py:496
  135.8 1.2 copy.18
  137.0 1.2 copy.19
  138.2 1.2 copy.20
  139.4 1.2 copy.21
  (1 shorter events, 0.0 us)

commit v2 on v0

v2 whole, which is shorter than its diff:
```python
import functools

import jax
import jax.numpy as jnp
from jax import lax
from jax.experimental import pallas as pl
from jax.experimental.pallas import tpu as pltpu
from jax.sharding import Mesh
from jax.sharding import PartitionSpec as P

SEQS = 8
TOPK = 20
EPS = 1e-06
NEG = -3.0e38
MESH = pl.DeviceIdType.MESH
CORE = "section"
AXES = ("x", "z", "y")
EVERY = (CORE,) + AXES
ORDERS = ((0, 1, 2), (1, 2, 0), (2, 0, 1))
N = 4


def pick(sel):
    return tuple(sel.get(i, slice(None)) for i in range(3))


def column_groups(width):
    tiles = width // 128
    cuts = [0, (tiles + 2) // 3, (2 * tiles + 2) // 3, tiles]
    waves = [[], []]
    for q in range(3):
        size = cuts[q + 1] - cuts[q]
        half = (size + 1) // 2 if q < 2 else size // 2 - (size // 2) % 2
        at = 128 * cuts[q]
        waves[0].append((at, 128 * half))
        waves[1].append((at + 128 * half, 128 * (size - half)))
    return waves


def toward(axis, k):
    name = AXES[axis]
    return {name: lax.rem(lax.axis_index(name) + k, N)}


def partner():
    return {CORE: 1 - lax.axis_index(CORE)}


def greet():
    barrier = pltpu.get_barrier_semaphore()
    for axis in range(3):
        for k in (1, 2, 3):
            pl.semaphore_signal(barrier, inc=1, device_id=toward(axis, k), device_id_type=MESH)
    pl.semaphore_signal(barrier, inc=1, device_id=partner(), device_id_type=MESH)


def met():
    pl.semaphore_wait(pltpu.get_barrier_semaphore(), 10)


class Mail:
    def __init__(self, send_sem, recv_sem):
        self.send_sem, self.recv_sem = send_sem, recv_sem
        self.copies, self.count = {}, 0

    def send(self, tag, src, dst, device):
        copy = pltpu.make_async_remote_copy(
            src_ref=src,
            dst_ref=dst,
            send_sem=self.send_sem.at[self.count],
            recv_sem=self.recv_sem.at[self.count],
            device_id=device,
            device_id_type=MESH,
        )
        copy.start()
        self.count += 1
        self.copies.setdefault(tag, []).append(copy)

    def received(self, tag):
        for copy in self.copies[tag]:
            copy.wait_recv()

    def all_sent(self):
        for copies in self.copies.values():
            for copy in copies:
                copy.wait_send()


WAVES = (0, 1)


def gather_start(buf, mail, groups):
    def go(s, q, tag, sel, axis):
        for k in (1, 3, 2):
            src, dst = dict(sel), dict(sel)
            src[axis], dst[axis] = 0, N - k
            rest = (slice(None), pl.ds(*groups[s][q]))
            mail.send((s, q, tag), buf.at[pick(src) + rest], buf.at[pick(dst) + rest], toward(axis, k))

    others = pl.ds(1, 3)
    every = [(s, q) + ORDERS[q] for s in WAVES for q in range(3)]
    for s, q, a, b, c in every:
        go(s, q, "a", {b: 0, c: 0}, a)
    for s, q, a, b, c in every:
        go(s, q, "b0", {a: 0, c: 0}, b)
    for s, q, a, b, c in every:
        go(s, q, "c0", {a: 0, b: 0}, c)
    for s, q, a, b, c in every:
        mail.received((s, q, "a"))
        go(s, q, "b1", {a: others, c: 0}, b)
    for s, q, a, b, c in every:
        go(s, q, "c1", {a: others, b: 0}, c)
    for s, q, a, b, c in every:
        mail.received((s, q, "b0"))
        go(s, q, "c2", {a: 0, b: others}, c)
    for s, q, a, b, c in every:
        mail.received((s, q, "b1"))
        go(s, q, "c3", {a: others, b: others}, c)


def gather_end(buf, out, mail, groups, s):
    for tag in ("c0", "c1", "c2", "c3"):
        for q in range(3):
            mail.received((s, q, tag))

    @pl.loop(0, N)
    def _(i):
        @pl.loop(0, N)
        def _(j):
            for k in range(N):
                for q in range(3):
                    cols = pl.ds(*groups[s][q])
                    out[i * N + j, pl.ds(4 * k, 4), cols] = buf[i, j, k, :, cols]


def rms(wide, gain):
    mean = jnp.mean(wide * wide, axis=-1, keepdims=True)
    return (wide * lax.rsqrt(mean + EPS) * gain).astype(jnp.bfloat16)


def by_tokens(weight, x, groups, s):
    rows = x.shape[0] * x.shape[1]
    total = None
    for q in range(3):
        cols = pl.ds(*groups[s][q])
        part = lax.dot_general(
            weight(cols), x[:, :, cols].reshape(rows, groups[s][q][1]), (((1,), (1,)), ((), ())),
            preferred_element_type=jnp.float32,
        )
        total = part if total is None else total + part
    return total


def order_ids(ids_ref, IDS, Q, V, own):
    Q[...] = jnp.zeros_like(Q)
    Q[0:2, :] = ids_ref[...].astype(jnp.float32)
    V[...] = Q[...].T
    size = ids_ref.shape[1]
    place = lax.broadcasted_iota(jnp.int32, (size, N**3 * 4), 1)
    row = lax.broadcasted_iota(jnp.int32, (size, N**3 * 4), 0)
    chip = jnp.zeros_like(place)
    for n, name in enumerate(AXES):
        chip = chip * N + lax.rem(lax.axis_index(name) + lax.rem(place // (4 * N ** (2 - n)), N), N)
    slot = (lax.axis_index(CORE) * N**3 + chip) * own + lax.rem(place, own)
    value = jnp.where(lax.rem(place, 4) // own == 0, V[:, 0:1], V[:, 1:2])
    IDS[...] = jnp.sum(jnp.where(row == slot, value, 0.0), axis=0, keepdims=True).astype(jnp.int32)


def sort_pairs(n):
    pairs, p = [], 1
    while p < n:
        k = p
        while k >= 1:
            for j in range(k % p, n - k, 2 * k):
                for i in range(min(k, n - j - k)):
                    if (i + j) // (2 * p) == (i + j + k) // (2 * p):
                        pairs.append((i + j, i + j + k))
            k //= 2
        p *= 2
    return pairs


def sort_down(values):
    values = list(values)
    for i, j in sort_pairs(len(values)):
        values[i], values[j] = jnp.maximum(values[i], values[j]), jnp.minimum(values[i], values[j])
    return values


def merge_down(left, right, keep=TOPK):
    left = list(left) + [False] * (keep - len(left))
    right = list(right) + [False] * (keep - len(right))

    def order(u, v):
        if u is None or v is False:
            return u, v
        if v is None or u is False:
            return v, u
        return jnp.maximum(u, v), jnp.minimum(u, v)

    line = [order(left[i], right[keep - 1 - i])[0] for i in range(keep)] + [None] * (32 - keep)
    gap = 16
    while gap:
        for i in range(32):
            if not i & gap:
                line[i], line[i + gap] = order(line[i], line[i + gap])
        gap //= 2
    return line[32 - keep :]


def slot_stats(LT, M, Q, V, IDS, ST, columns):
    levels, rows = 16, LT.shape[1]
    deep = LT.shape[0] // levels
    chip = (lax.axis_index("x") * N + lax.axis_index("z")) * N + lax.axis_index("y")
    core = lax.axis_index(CORE)
    first = (core * N**3 + chip) * columns
    second = ((1 - core) * N**3 + chip) * columns
    for t in range(rows // 128):
        lanes = pl.ds(128 * t, 128)
        ids = IDS[:, lanes]

        @pl.loop(0, deep // 16)
        def _(j):
            both = []
            for side in range(2):
                at = pl.multiple_of(side * (deep // 2) + j * 8, 8)
                both.append(sort_down([LT[pl.ds(l * deep + at, 8), lanes] for l in range(levels)]))
            for l, value in enumerate(merge_down(*both)):
                M[l, pl.ds(pl.multiple_of(j * 8, 8), 8), lanes] = value

        have = deep // 16
        while have > 1:
            have //= 2

            @pl.loop(0, have)
            def _(j):
                both = []
                for side in range(2):
                    at = pl.multiple_of((side * have + j) * 8, 8)
                    both.append([M[l, pl.ds(at, 8), lanes] for l in range(TOPK)])
                for l, value in enumerate(merge_down(*both)):
                    M[l, pl.ds(pl.multiple_of(j * 8, 8), 8), lanes] = value

        top = [M[l, pl.ds(0, 8), lanes] for l in range(TOPK)]
        for shift in (4, 2, 1):
            top = merge_down(top, [pltpu.roll(v, shift, 0) for v in top])
        peak = top[0]

        def body(j, carry):
            total, hit = carry
            at = pl.multiple_of(j * 8, 8)
            value = LT[pl.ds(at, 8), lanes]
            row = lax.broadcasted_iota(jnp.int32, (8, 128), 0) + at
            late = row >= LT.shape[0] // 2
            column = jnp.where(late, row - LT.shape[0] // 2, row)
            token = column + jnp.where(late, second, first)
            same = (token == ids) & (column < columns)
            return total + jnp.exp(value - peak), hit + jnp.where(same, value, 0.0)

        zero = jnp.zeros((8, 128), jnp.float32)
        total, hit = lax.fori_loop(0, LT.shape[0] // 8, body, (zero, zero), unroll=8)
        for l in range(TOPK):
            Q[pl.ds(l, 1), lanes] = top[l][0:1]
        Q[pl.ds(TOPK, 1), lanes] = jnp.sum(total, axis=0, keepdims=True)
        Q[pl.ds(TOPK + 1, 1), lanes] = jnp.sum(hit, axis=0, keepdims=True)
    V[...] = Q[...].T
    for i in range(N):
        for j in range(N):
            for k in range(N):
                ST[i, j, k] = V[pl.ds(((i * N + j) * N + k) * 4, 4), :]


def merged(U3, V, Q):
    for i in range(N):
        for j in range(N):
            for k in range(N):
                V[pl.ds(((i * N + j) * N + k) * 4, 4), :] = U3[i, j, k]
    Q[...] = V[...].T

    def line(l):
        return [Q[pl.ds(l, 1), pl.ds(128 * t, 128)] for t in range(2)]

    lists = [line(l) for l in range(TOPK)]
    top = merge_down([v[0] for v in lists], [v[1] for v in lists])
    for shift in (64, 32, 16, 8, 4):
        top = merge_down(top, [pltpu.roll(v, shift, 1) for v in top])
    peak = top[0]
    sums, hits = line(TOPK), line(TOPK + 1)
    total = sum(s * jnp.exp(v - peak) for s, v in zip(sums, lists[0]))
    hit = hits[0] + hits[1]
    for shift in (64, 32, 16, 8, 4):
        total = total + pltpu.roll(total, shift, 1)
        hit = hit + pltpu.roll(hit, shift, 1)
    log_norm = peak + jnp.log(total)
    mass = sum(jnp.exp(v - log_norm) for v in top)
    return hit - log_norm, log_norm, mass


def by_sequence(logprob, sid_ref):
    lane = lax.broadcasted_iota(jnp.int32, (1, 128), 1)
    turned = [logprob] + [pltpu.roll(logprob, j, 1) for j in (1, 2, 3)]
    part = jnp.zeros((1, 128), jnp.float32)
    for t in range(4):
        spread = turned[0]
        for j in (1, 2, 3):
            spread = jnp.where(lax.rem(lane - t + 4, 4) == j, turned[j], spread)
        mine = (lane // SEQS == t // 2) & (lax.rem(lane, SEQS) == sid_ref[t // 2, t % 2])
        part = part + jnp.where(mine, spread, 0.0)
    return jnp.broadcast_to(part, (8, 128))


def score_kernel(
    h_ref, gf_ref, gl_ref, wg_ref, wu_ref, wd_ref, hw_ref, ids_ref, sid_ref,
    out_ref,
    HS, G, X, S, R1, R2, R3, T1, T2, F, PB, W, WD, Y, ACT, HB, LT, M, Q, V, IDS, ST, U1, U2, U3, A,
    own_s, swap_s, swap_r, g_s, g_r, r_s, r_r, g2_s, g2_r, a_s, a_r, q_s, q_r,
):
    width = h_ref.shape[-1]
    groups = column_groups(width)
    rows = N**3 * 4
    hidden = W.shape[1]
    columns = HB.shape[1]
    loads = []
    for n, (src, dst) in enumerate(((wg_ref, W.at[0]), (wu_ref, W.at[1]), (wd_ref, WD.at[0]))):
        copy = pltpu.make_async_copy(src, dst, own_s.at[n])
        copy.start()
        loads.append(copy)
    greet()
    own = h_ref.shape[1]
    for m in range(h_ref.shape[0]):
        HS[pl.ds(m * own, own), :] = h_ref[m].astype(jnp.float32)
    G[0, 0, 0] = rms(HS[...], gf_ref[...])
    met()
    mail = Mail(g_s, g_r)
    swap = Mail(swap_s, swap_r)
    for tag, src, dst in (("g", wg_ref, W.at[2]), ("u", wu_ref, W.at[3]), ("d", wd_ref, WD.at[1])):
        swap.send(tag, src, dst, partner())
    gather_start(G, mail, groups)
    order_ids(ids_ref, IDS, Q, V, own)
    for copy in loads[:2]:
        copy.wait()
    for tag in ("g", "u"):
        swap.received(tag)
    for s in WAVES:
        gather_end(G, X, mail, groups, s)
        part = by_tokens(lambda cols: W[:, :, cols].reshape(4 * hidden, cols.size), X, groups, s)
        Y[...] = part if s == 0 else Y[...] + part
    loads[2].wait()
    swap.received("d")
    swap.send("h", hw_ref, HB.at[1], partner())
    own_head = pltpu.make_async_copy(hw_ref, HB.at[0], own_s.at[3])
    own_head.start()
    acts = []
    for p in range(2):
        gate, up = Y[pl.ds(2 * p * hidden, hidden), :], Y[pl.ds((2 * p + 1) * hidden, hidden), :]
        acts.append(gate / (1.0 + jnp.exp(-gate)) * up)
    ACT[...] = jnp.concatenate(acts, axis=0).T.astype(jnp.bfloat16)
    mail.all_sent()

    red = Mail(r_s, r_r)
    wide = PB.shape[-1]

    def down(at, size):
        cols = pl.ds(at, size)
        part = jnp.dot(ACT[...], WD[:, :, cols].reshape(2 * hidden, size), preferred_element_type=jnp.float32)
        PB[:, :, pl.ds(0, size)] = part.astype(jnp.bfloat16).reshape(N * N, N * 4, size)
        for i in range(N):
            for j in range(N):
                for k in range(N):
                    S[i, j, k, :, cols] = PB[i * N + j, pl.ds(4 * k, 4), pl.ds(0, size)]

    every = [(s, q, pl.ds(*groups[s][q])) + ORDERS[q] for s in WAVES for q in range(3)]
    for s, q, cols, a, b, c in every:
        start, size = groups[s][q]

        @pl.loop(0, size // wide)
        def _(n):
            down(pl.multiple_of(start + n * wide, 128), wide)

        if size % wide:
            down(start + size // wide * wide, size % wide)
        rest = (slice(None), cols)
        for k in (2, 1, 3):
            red.send((s, q, 1), S.at[pick({c: k}) + rest], R1.at[(k - 1, slice(None), slice(None)) + rest], toward(c, k))
    for s, q, cols, a, b, c in every:
        red.received((s, q, 1))

        @pl.loop(0, N)
        def _(i):
            @pl.loop(0, N)
            def _(j):
                left = [i, j]
                sel = {ax: left.pop(0) for ax in range(3) if ax != c}
                sel[c] = 0
                total = S[pick(sel) + (slice(None), cols)].astype(jnp.float32)
                for k in range(3):
                    total += R1[k, i, j, :, cols].astype(jnp.float32)
                T1[i, j, :, cols] = total.astype(jnp.bfloat16)

        first = min(a, b)
        for k in (2, 1, 3):
            src = T1.at[k, :, :, cols] if b == first else T1.at[:, k, :, cols]
            red.send((s, q, 2), src, R2.at[k - 1, :, :, cols], toward(b, k))
    for s, q, cols, a, b, c in every:
        red.received((s, q, 2))
        first = min(a, b)
        for i in range(N):
            total = (T1[0, i, :, cols] if b == first else T1[i, 0, :, cols]).astype(jnp.float32)
            for k in range(3):
                total += R2[k, i, :, cols].astype(jnp.float32)
            T2[i, :, cols] = total.astype(jnp.bfloat16)
        for k in (2, 1, 3):
            red.send((s, q, 3), T2.at[k, :, cols], R3.at[k - 1, :, cols], toward(a, k))
    for s, q, cols, a, b, c in every:
        red.received((s, q, 3))
        total = T2[0, :, cols].astype(jnp.float32)
        for k in range(3):
            total += R3[k, :, cols].astype(jnp.float32)
        F[:, cols] = total

    residual = (HS[...] + F[...]).astype(jnp.bfloat16)
    G[0, 0, 0] = rms(residual.astype(jnp.float32), gl_ref[...])
    mail2 = Mail(g2_s, g2_r)
    gather_start(G, mail2, groups)
    swap.received("h")
    own_head.wait()
    half, tall = LT.shape[0] // 2, 256
    for s in WAVES:
        gather_end(G, X, mail2, groups, s)
        for p in range(2):
            if s == 0:
                LT[pl.ds(p * half + columns // 8 * 8, half - columns // 8 * 8), :] = jnp.full(
                    (half - columns // 8 * 8, rows), NEG, jnp.float32
                )

            def logits(at, size):
                part = by_tokens(lambda cols: HB[p, pl.ds(at, size), cols], X, groups, s)
                to = pl.ds(p * half + at, size)
                LT[to, :] = part if s == 0 else LT[to, :] + part

            @pl.loop(0, columns // tall)
            def _(n):
                logits(pl.multiple_of(n * tall, tall), tall)

            if columns % tall:
                logits(columns // tall * tall, columns % tall)

    slot_stats(LT, M, Q, V, IDS, ST, columns)

    stats = Mail(a_s, a_r)
    for k in (2, 1, 3):
        stats.send(1, ST.at[:, :, k], U1.at[N - k], toward(2, k))
    U1[0] = ST[:, :, 0]
    stats.received(1)
    for k in (2, 1, 3):
        stats.send(2, U1.at[:, :, k], U2.at[N - k], toward(1, k))
    U2[0] = U1[:, :, 0]
    stats.received(2)
    for k in (2, 1, 3):
        stats.send(3, U2.at[:, :, k], U3.at[N - k], toward(0, k))
    U3[0] = U2[:, :, 0]
    stats.received(3)
    logprob, log_norm, mass = merged(U3, V, Q)

    A[0, 0] = by_sequence(logprob, sid_ref)
    seq = Mail(q_s, q_r)
    seq.send(0, A.at[0, 0], A.at[0, 1], partner())
    seq.received(0)
    both = A[0, 0] + A[0, 1]
    for axis in range(3):
        A[axis + 1, 0] = both
        for k in (2, 1, 3):
            seq.send(axis + 1, A.at[axis + 1, 0], A.at[axis + 1, N - k], toward(axis, k))
        seq.received(axis + 1)
        got = [A[axis + 1, k] for k in range(N)]
        both = (got[0] + got[2]) + (got[1] + got[3])
    for n, value in enumerate((logprob, log_norm, mass, both[0:1])):
        out_ref[pl.ds(n, 1), :] = value
    out_ref[4:8, :] = jnp.zeros((4, 128), jnp.float32)
    for m in (swap, red, mail2, stats, seq):
        m.all_sent()


def score(h, gain_ffn, gain_final, w_gate, w_up, w_down, head, ids, seq_ids):
    hidden, width = w_gate.shape
    columns = head.shape[0]
    half = -(-columns // 256) * 256
    rows = N**3 * 4
    bf16, f32 = jnp.bfloat16, jnp.float32
    vmem, anywhere = pl.BlockSpec(memory_space=pltpu.VMEM), pl.BlockSpec(memory_space=pl.ANY)
    dma = lambda n: pltpu.SemaphoreType.DMA((n,))
    stat = pltpu.VMEM((N, N, N, 4, 128), f32)
    return pl.pallas_call(
        score_kernel,
        out_shape=jax.ShapeDtypeStruct((8, 128), f32),
        in_specs=[vmem, vmem, vmem, anywhere, anywhere, anywhere, anywhere, vmem, pl.BlockSpec(memory_space=pltpu.SMEM)],
        out_specs=vmem,
        scratch_shapes=[
            pltpu.VMEM((4, width), f32),
            pltpu.VMEM((N, N, N, 4, width), bf16),
            pltpu.VMEM((N * N, N * 4, width), bf16),
            pltpu.VMEM((N, N, N, 4, width), bf16),
            pltpu.VMEM((3, N, N, 4, width), bf16),
            pltpu.VMEM((3, N, 4, width), bf16),
            pltpu.VMEM((3, 4, width), bf16),
            pltpu.VMEM((N, N, 4, width), bf16),
            pltpu.VMEM((N, 4, width), bf16),
            pltpu.VMEM((4, width), f32),
            pltpu.VMEM((N * N, N * 4, 256), bf16),
            pltpu.VMEM((4, hidden, width), bf16),
            pltpu.VMEM((2, hidden, width), bf16),
            pltpu.VMEM((4 * hidden, rows), f32),
            pltpu.VMEM((rows, 2 * hidden), bf16),
            pltpu.VMEM((2, columns, width), bf16),
            pltpu.VMEM((2 * half, rows), f32),
            pltpu.VMEM((TOPK, half // 16, rows), f32),
            pltpu.VMEM((128, rows), f32),
            pltpu.VMEM((rows, 128), f32),
            pltpu.VMEM((1, rows), jnp.int32),
            stat, stat, stat, stat,
            pltpu.VMEM((4, N, 8, 128), f32),
            dma(4), dma(4), dma(4), dma(126), dma(126), dma(54), dma(54), dma(126), dma(126), dma(9), dma(9), dma(10), dma(10),
        ],
        compiler_params=pltpu.CompilerParams(collective_id=0, has_side_effects=True, vmem_limit_bytes=67043328),
        name="score",
    )(h, gain_ffn, gain_final, w_gate, w_up, w_down, head, ids, seq_ids)


def emit_kernel(x_ref, lp_ref, ln_ref, tm_ref, sq_ref):
    for n, ref in enumerate((lp_ref, ln_ref, tm_ref, sq_ref)):
        size = ref.shape[1]
        line = x_ref[pl.ds(n, 1), :]
        ref[0:1, :] = line[:, 0:size]
        ref[1:2, :] = pltpu.roll(line, 128 - size, 1)[:, 0:size]


def emit(x, own):
    f32 = jnp.float32
    small = jax.ShapeDtypeStruct((2, own), f32)
    return pl.pallas_call(
        emit_kernel, out_shape=(small, small, small, jax.ShapeDtypeStruct((2, SEQS), f32)), name="emit"
    )(x)


def body(hidden_in, gain_ffn, w_gate, w_up, w_down, gain_final, head_weight, sampled_ids, seq_ids):
    width = hidden_in.shape[-1]
    packed = score(
        hidden_in, gain_ffn.reshape(1, width), gain_final.reshape(1, width),
        w_gate.T, w_up.T, w_down, head_weight.T, sampled_ids, seq_ids,
    )
    return tuple(emit(packed, hidden_in.shape[1]))


def solution(mesh):
    split = Mesh(mesh.devices.reshape(mesh.shape["section"], N, N, N), EVERY)
    rows = P(None, EVERY)
    return jax.shard_map(
        body,
        mesh=split,
        in_specs=(P(None, EVERY, None), P(), rows, rows, P(EVERY, None), P(), rows, P(), rows),
        out_specs=(rows, rows, rows, P()),
        check_vma=False,
    )
```

time: 678 us -> 121 us (0.18); the launches traced: 669 us -> 121 us
  waiting for transfers between devices: 307 us -> 0 us
  other arithmetic: 178 us -> 0 us
  Pallas kernels: 0 us -> 120 us
  blocking collectives: 109 us -> 0 us
  matrix products: 42.3 us -> 0 us
  local copies, waits for them, and re-layouts: 18 us -> 0 us
  between operations: 15.2 us -> 0.64 us
    psum x1 -> x0, waiting for transfers between devices: 171 us -> none  [body(): lax.psum(jnp.dot(hidden_act, w_down, preferred_element_type=jnp.float32),...]
    sort x22 -> x0, other arithmetic: 154 us -> none  [largest(): return lax.sort(values, dimension=values.ndim - 1)[..., -TOPK:]]
    all_gather x2 -> x0, waiting for transfers between devices: 136 us -> none  [body(): gathered = lax.all_gather(own_rows, SECTION_VOCAB, axis=0, tiled=True)]
    pallas_call x0 -> x2, Pallas kernels: none -> 120 us  [the longest x1 119 us: score(): pl.pallas_call(score_kernel, out_shape=jax.ShapeDtypeStruct((8, 128), f32...]
    all_gather x8 -> x0, blocking collectives: 76.4 us -> none  [collected_together(): both, at, found = (lax.all_gather(jnp.concatenate(lines), axis), 0, {})]
    dot_general x6 -> x0, matrix products: 42.3 us -> none  [the longest x2 20.1 us: body(): jnp.dot(hidden_act, w_down, preferred_element_type=jnp.float32)]
    psum x4 -> x0, blocking collectives: 32.3 us -> none  [over_axes(): shard = lax.psum(shard, axis)]
    reduce_sum x8 -> x0, other arithmetic: 20.8 us -> none  [the longest x3 20 us: rms_norm(): square_mean = jnp.mean(wide * wide, axis=-1, keepdims=True)]
  transfers between devices with their start and end apart: 3 -> 0, of which waited for: 3 -> 0; matrix products, arithmetic and copies ran while one was open for 1% -> 0% of each run, Pallas kernels for 0% -> 0%
where the time goes in v2:
time: 121 us
  Pallas kernels  120 us (99%)
    pallas_call x1, Pallas kernels, score(): pl.pallas_call(score_kernel, out_shape=jax.ShapeDtypeStruct((8, 128), f32...  119 us

profile of v2, /device:TPU:0, one launch (start us, length us, event | category | flops | bytes accessed | tf_op | source)
XLA Modules:
  0.0 121.1 jit_solution(15579213641593784514)
XLA Ops:
  0.6 119.2 %score.1.x_ref = f32[8,128]{1,0:T(8,128)} custom-call(bf16[2,2,7168]{2,1,0:T(2,128)(2,1)} %h_ref.1, f32[1,7168]{1,0:T(1,128)} %bitcast.8, f32[1,7168]{1,0:T(1,128)} %bitcast.9, bf16[144,7168]{1,0:T(8,128)(2,1)} %bitcast.6, bf16[144,7168]{1,0:T(8,128)(2,1)} %bitcast.7, bf16[144,7168]{1,0:T(8,128)(2,1)} %wd_ref.1, bf16[1010,7168]{1,0:T(8,128)(2,1)} %bitcast.5, ...), custom_call_target="tpu_custom_call" | custom-call | tf_op jit(solution)/shard_map/score/pallas_call | solution.py:493
  119.8 1.3 %emit.1 = (f32[2,2]{1,0:T(2,128)}, f32[2,2]{1,0:T(2,128)}, f32[2,2]{1,0:T(2,128)}, f32[2,8]{1,0:T(2,128)}) custom-call(f32[8,128]{1,0:T(8,128)} %score.1.x_ref), custom_call_target="tpu_custom_call" | custom-call | tf_op jit(solution)/shard_map/emit/pallas_call | solution.py:540

commit v3 on v2

--- a/solution.py
+++ b/solution.py
@@ -98,24 +98,27 @@
             mail.send((s, q, tag), buf.at[pick(src) + rest], buf.at[pick(dst) + rest], toward(axis, k))
 
     others = pl.ds(1, 3)
-    every = [(s, q) + ORDERS[q] for s in WAVES for q in range(3)]
-    for s, q, a, b, c in every:
-        go(s, q, "a", {b: 0, c: 0}, a)
-    for s, q, a, b, c in every:
-        go(s, q, "b0", {a: 0, c: 0}, b)
-    for s, q, a, b, c in every:
-        go(s, q, "c0", {a: 0, b: 0}, c)
-    for s, q, a, b, c in every:
-        mail.received((s, q, "a"))
-        go(s, q, "b1", {a: others, c: 0}, b)
-    for s, q, a, b, c in every:
-        go(s, q, "c1", {a: others, b: 0}, c)
-    for s, q, a, b, c in every:
-        mail.received((s, q, "b0"))
-        go(s, q, "c2", {a: 0, b: others}, c)
-    for s, q, a, b, c in every:
-        mail.received((s, q, "b1"))
-        go(s, q, "c3", {a: others, b: others}, c)
+    def each(s, tag, sel, along, after=None):
+        for q, axes in enumerate(ORDERS):
+            named = dict(zip("abc", axes))
+            if after:
+                mail.received((s, q, after))
+            go(s, q, tag, {named[n]: v for n, v in sel.items()}, named[along])
+
+    for s in WAVES:
+        each(s, "a", {"b": 0, "c": 0}, "a")
+        each(s, "b0", {"a": 0, "c": 0}, "b")
+    each(0, "c0", {"a": 0, "b": 0}, "c")
+    for s in WAVES:
+        each(s, "b1", {"a": others, "c": 0}, "b", "a")
+        if s == 0:
+            each(s, "c1", {"a": others, "b": 0}, "c")
+    each(0, "c2", {"a": 0, "b": others}, "c", "b0")
+    each(0, "c3", {"a": others, "b": others}, "c", "b1")
+    each(1, "c0", {"a": 0, "b": 0}, "c")
+    each(1, "c1", {"a": others, "b": 0}, "c")
+    each(1, "c2", {"a": 0, "b": others}, "c", "b0")
+    each(1, "c3", {"a": others, "b": others}, "c", "b1")
 
 
 def gather_end(buf, out, mail, groups, s):
@@ -208,7 +211,18 @@
     return line[32 - keep :]
 
 
-def slot_stats(LT, M, Q, V, IDS, ST, columns):
+def away(i, j, k):
+    offsets = (i, j, k)
+    return {name: lax.rem(lax.axis_index(name) + offsets[n], N) for n, name in enumerate(AXES)}
+
+
+FAR = sorted(
+    ((i, j, k) for i in range(N) for j in range(N) for k in range(N)),
+    key=lambda at: -sum(min(v, N - v) for v in at),
+)
+
+
+def slot_stats(LT, M, Q, V, IDS, ST, U, mail, columns):
     levels, rows = 16, LT.shape[1]
     deep = LT.shape[0] // levels
     chip = (lax.axis_index("x") * N + lax.axis_index("z")) * N + lax.axis_index("y")
@@ -263,18 +277,23 @@
             Q[pl.ds(l, 1), lanes] = top[l][0:1]
         Q[pl.ds(TOPK, 1), lanes] = jnp.sum(total, axis=0, keepdims=True)
         Q[pl.ds(TOPK + 1, 1), lanes] = jnp.sum(hit, axis=0, keepdims=True)
-    V[...] = Q[...].T
+        V[lanes, :] = Q[:, lanes].T
+        for at in FAR:
+            i, j, k = at
+            if (i * N**2 + j * N + k) * 4 // 128 == t:
+                to = U if at == (0, 0, 0) else ST
+                to[i, j, k] = V[pl.ds(((i * N + j) * N + k) * 4, 4), :]
+        for at in FAR[:-1]:
+            i, j, k = at
+            if (i * N**2 + j * N + k) * 4 // 128 == t:
+                mail.send(0, ST.at[i, j, k], U.at[(N - i) % N, (N - j) % N, (N - k) % N], away(i, j, k))
+
+
+def merged(U, V, Q):
     for i in range(N):
         for j in range(N):
             for k in range(N):
-                ST[i, j, k] = V[pl.ds(((i * N + j) * N + k) * 4, 4), :]
-
-
-def merged(U3, V, Q):
-    for i in range(N):
-        for j in range(N):
-            for k in range(N):
-                V[pl.ds(((i * N + j) * N + k) * 4, 4), :] = U3[i, j, k]
+                V[pl.ds(((i * N + j) * N + k) * 4, 4), :] = U[i, j, k]
     Q[...] = V[...].T
 
     def line(l):
@@ -306,13 +325,13 @@
             spread = jnp.where(lax.rem(lane - t + 4, 4) == j, turned[j], spread)
         mine = (lane // SEQS == t // 2) & (lax.rem(lane, SEQS) == sid_ref[t // 2, t % 2])
         part = part + jnp.where(mine, spread, 0.0)
-    return jnp.broadcast_to(part, (8, 128))
+    return part
 
 
 def score_kernel(
     h_ref, gf_ref, gl_ref, wg_ref, wu_ref, wd_ref, hw_ref, ids_ref, sid_ref,
     out_ref,
-    HS, G, X, S, R1, R2, R3, T1, T2, F, PB, W, WD, Y, ACT, HB, LT, M, Q, V, IDS, ST, U1, U2, U3, A,
+    HS, G, X, S, R1, R2, R3, T1, T2, F, PB, W, WD, Y, ACT, HB, LT, M, Q, V, IDS, ST, U, A, B,
     own_s, swap_s, swap_r, g_s, g_r, r_s, r_r, g2_s, g2_r, a_s, a_r, q_s, q_r,
 ):
     width = h_ref.shape[-1]
@@ -358,7 +377,6 @@
     mail.all_sent()
 
     red = Mail(r_s, r_r)
-    wide = PB.shape[-1]
 
     def down(at, size):
         cols = pl.ds(at, size)
@@ -373,12 +391,7 @@
     for s, q, cols, a, b, c in every:
         start, size = groups[s][q]
 
-        @pl.loop(0, size // wide)
-        def _(n):
-            down(pl.multiple_of(start + n * wide, 128), wide)
-
-        if size % wide:
-            down(start + size // wide * wide, size % wide)
+        down(start, size)
         rest = (slice(None), cols)
         for k in (2, 1, 3):
             red.send((s, q, 1), S.at[pick({c: k}) + rest], R1.at[(k - 1, slice(None), slice(None)) + rest], toward(c, k))
@@ -424,7 +437,7 @@
     gather_start(G, mail2, groups)
     swap.received("h")
     own_head.wait()
-    half, tall = LT.shape[0] // 2, 256
+    half, tall = LT.shape[0] // 2, 512
     for s in WAVES:
         gather_end(G, X, mail2, groups, s)
         for p in range(2):
@@ -438,43 +451,28 @@
                 to = pl.ds(p * half + at, size)
                 LT[to, :] = part if s == 0 else LT[to, :] + part
 
-            @pl.loop(0, columns // tall)
-            def _(n):
-                logits(pl.multiple_of(n * tall, tall), tall)
-
-            if columns % tall:
-                logits(columns // tall * tall, columns % tall)
-
-    slot_stats(LT, M, Q, V, IDS, ST, columns)
+            for at in range(0, columns, tall):
+                logits(at, min(tall, columns - at))
 
     stats = Mail(a_s, a_r)
-    for k in (2, 1, 3):
-        stats.send(1, ST.at[:, :, k], U1.at[N - k], toward(2, k))
-    U1[0] = ST[:, :, 0]
-    stats.received(1)
-    for k in (2, 1, 3):
-        stats.send(2, U1.at[:, :, k], U2.at[N - k], toward(1, k))
-    U2[0] = U1[:, :, 0]
-    stats.received(2)
-    for k in (2, 1, 3):
-        stats.send(3, U2.at[:, :, k], U3.at[N - k], toward(0, k))
-    U3[0] = U2[:, :, 0]
-    stats.received(3)
-    logprob, log_norm, mass = merged(U3, V, Q)
-
-    A[0, 0] = by_sequence(logprob, sid_ref)
+    slot_stats(LT, M, Q, V, IDS, ST, U, stats, columns)
+    stats.received(0)
+    logprob, log_norm, mass = merged(U, V, Q)
+
+    A[0] = by_sequence(logprob, sid_ref)
     seq = Mail(q_s, q_r)
-    seq.send(0, A.at[0, 0], A.at[0, 1], partner())
+    seq.send(0, A.at[0], A.at[1], partner())
     seq.received(0)
-    both = A[0, 0] + A[0, 1]
-    for axis in range(3):
-        A[axis + 1, 0] = both
-        for k in (2, 1, 3):
-            seq.send(axis + 1, A.at[axis + 1, 0], A.at[axis + 1, N - k], toward(axis, k))
-        seq.received(axis + 1)
-        got = [A[axis + 1, k] for k in range(N)]
-        both = (got[0] + got[2]) + (got[1] + got[3])
-    for n, value in enumerate((logprob, log_norm, mass, both[0:1])):
+    B[0, 0, 0] = A[0] + A[1]
+    for i, j, k in FAR[:-1]:
+        seq.send(1, B.at[0, 0, 0], B.at[(N - i) % N, (N - j) % N, (N - k) % N], away(i, j, k))
+    seq.received(1)
+
+    def joined(values):
+        return (values[0] + values[2]) + (values[1] + values[3])
+
+    both = joined([joined([joined([B[i, j, k] for i in range(N)]) for j in range(N)]) for k in range(N)])
+    for n, value in enumerate((logprob, log_norm, mass, both)):
         out_ref[pl.ds(n, 1), :] = value
     out_ref[4:8, :] = jnp.zeros((4, 128), jnp.float32)
     for m in (swap, red, mail2, stats, seq):
@@ -506,7 +504,7 @@
             pltpu.VMEM((N, N, 4, width), bf16),
             pltpu.VMEM((N, 4, width), bf16),
             pltpu.VMEM((4, width), f32),
-            pltpu.VMEM((N * N, N * 4, 256), bf16),
+            pltpu.VMEM((N * N, N * 4, 1280), bf16),
             pltpu.VMEM((4, hidden, width), bf16),
             pltpu.VMEM((2, hidden, width), bf16),
             pltpu.VMEM((4 * hidden, rows), f32),
@@ -517,9 +515,10 @@
             pltpu.VMEM((128, rows), f32),
             pltpu.VMEM((rows, 128), f32),
             pltpu.VMEM((1, rows), jnp.int32),
-            stat, stat, stat, stat,
-            pltpu.VMEM((4, N, 8, 128), f32),
-            dma(4), dma(4), dma(4), dma(126), dma(126), dma(54), dma(54), dma(126), dma(126), dma(9), dma(9), dma(10), dma(10),
+            stat, stat,
+            pltpu.VMEM((2, 1, 128), f32),
+            pltpu.VMEM((N, N, N, 1, 128), f32),
+            dma(4), dma(4), dma(4), dma(126), dma(126), dma(54), dma(54), dma(126), dma(126), dma(63), dma(63), dma(64), dma(64),
         ],
         compiler_params=pltpu.CompilerParams(collective_id=0, has_side_effects=True, vmem_limit_bytes=67043328),
         name="score",

time: 121 us -> 111 us (0.917); the launches traced: 121 us -> 110 us
  Pallas kernels: 120 us -> 109 us
    pallas_call x1, Pallas kernels: 119 us -> 108 us  [score(): pl.pallas_call(score_kernel, out_shape=jax.ShapeDtypeStruct((8, 128), f32...]
where the time goes in v3:
time: 111 us; the launch traced here: 110 us
  Pallas kernels  109 us (98%)
    pallas_call x1, Pallas kernels, score(): pl.pallas_call(score_kernel, out_shape=jax.ShapeDtypeStruct((8, 128), f32...  108 us

profile of v3, /device:TPU:0, one launch (start us, length us, event | category | flops | bytes accessed | tf_op | source)
XLA Modules:
  0.0 109.7 jit_solution(2332829467635291430)
XLA Ops:
  0.6 107.7 %score.1.x_ref = f32[8,128]{1,0:T(8,128)} custom-call(bf16[2,2,7168]{2,1,0:T(2,128)(2,1)} %h_ref.1, f32[1,7168]{1,0:T(1,128)} %bitcast.8, f32[1,7168]{1,0:T(1,128)} %bitcast.9, bf16[144,7168]{1,0:T(8,128)(2,1)} %bitcast.6, bf16[144,7168]{1,0:T(8,128)(2,1)} %bitcast.7, bf16[144,7168]{1,0:T(8,128)(2,1)} %wd_ref.1, bf16[1010,7168]{1,0:T(8,128)(2,1)} %bitcast.5, ...), custom_call_target="tpu_custom_call" | custom-call | tf_op jit(solution)/shard_map/score/pallas_call | solution.py:491
  108.4 1.3 %emit.1 = (f32[2,2]{1,0:T(2,128)}, f32[2,2]{1,0:T(2,128)}, f32[2,2]{1,0:T(2,128)}, f32[2,8]{1,0:T(2,128)}) custom-call(f32[8,128]{1,0:T(8,128)} %score.1.x_ref), custom_call_target="tpu_custom_call" | custom-call | tf_op jit(solution)/shard_map/emit/pallas_call | solution.py:539

commit v4 on v3

--- a/solution.py
+++ b/solution.py
@@ -46,6 +46,17 @@
     return {CORE: 1 - lax.axis_index(CORE)}
 
 
+def away(i, j, k):
+    offsets = (i, j, k)
+    return {name: lax.rem(lax.axis_index(name) + offsets[n], N) for n, name in enumerate(AXES)}
+
+
+FAR = sorted(
+    ((i, j, k) for i in range(N) for j in range(N) for k in range(N)),
+    key=lambda at: -sum(min(v, N - v) for v in at),
+)
+
+
 def greet():
     barrier = pltpu.get_barrier_semaphore()
     for axis in range(3):
@@ -61,64 +72,90 @@
 class Mail:
     def __init__(self, send_sem, recv_sem):
         self.send_sem, self.recv_sem = send_sem, recv_sem
-        self.copies, self.count = {}, 0
-
-    def send(self, tag, src, dst, device):
-        copy = pltpu.make_async_remote_copy(
+        self.wholes, self.places = {}, {}
+
+    def send(self, tag, whole, src, dst, device):
+        place = self.places.setdefault(tag, len(self.places))
+        self.wholes[tag] = whole
+        pltpu.make_async_remote_copy(
             src_ref=src,
             dst_ref=dst,
-            send_sem=self.send_sem.at[self.count],
-            recv_sem=self.recv_sem.at[self.count],
+            send_sem=self.send_sem.at[place],
+            recv_sem=self.recv_sem.at[place],
             device_id=device,
             device_id_type=MESH,
+        ).start()
+
+    def all_of(self, tag):
+        place, whole = self.places[tag], self.wholes[tag]
+        return pltpu.make_async_remote_copy(
+            src_ref=whole,
+            dst_ref=whole,
+            send_sem=self.send_sem.at[place],
+            recv_sem=self.recv_sem.at[place],
+            device_id=partner(),
+            device_id_type=MESH,
         )
-        copy.start()
-        self.count += 1
-        self.copies.setdefault(tag, []).append(copy)
 
     def received(self, tag):
-        for copy in self.copies[tag]:
-            copy.wait_recv()
+        self.all_of(tag).wait_recv()
 
     def all_sent(self):
-        for copies in self.copies.values():
-            for copy in copies:
-                copy.wait_send()
+        for tag in self.places:
+            self.all_of(tag).wait_send()
+
+    def spread(self, src, dst, only=None):
+        some = pl.ds(1, 3)
+        wholes = (dst.at[some], dst.at[0, some], dst.at[0, 0, some])
+        for at in FAR[:-1]:
+            if only is None or only(at):
+                tag = 0 if at[0] else 1 if at[1] else 2
+                self.send(tag, wholes[tag], src(*at), dst.at[tuple((N - v) % N for v in at)], away(*at))
+
+    def all_received(self):
+        for tag in self.places:
+            self.received(tag)
 
 
 WAVES = (0, 1)
 
 
-def gather_start(buf, mail, groups):
-    def go(s, q, tag, sel, axis):
-        for k in (1, 3, 2):
-            src, dst = dict(sel), dict(sel)
-            src[axis], dst[axis] = 0, N - k
-            rest = (slice(None), pl.ds(*groups[s][q]))
-            mail.send((s, q, tag), buf.at[pick(src) + rest], buf.at[pick(dst) + rest], toward(axis, k))
-
-    others = pl.ds(1, 3)
-    def each(s, tag, sel, along, after=None):
+class Gather:
+    def __init__(self, buf, mail, groups):
+        self.buf, self.mail, self.groups = buf, mail, groups
+
+    def each(self, s, tag, sel, along, after=None):
         for q, axes in enumerate(ORDERS):
             named = dict(zip("abc", axes))
+            axis = named[along]
             if after:
-                mail.received((s, q, after))
-            go(s, q, tag, {named[n]: v for n, v in sel.items()}, named[along])
-
-    for s in WAVES:
-        each(s, "a", {"b": 0, "c": 0}, "a")
-        each(s, "b0", {"a": 0, "c": 0}, "b")
-    each(0, "c0", {"a": 0, "b": 0}, "c")
-    for s in WAVES:
-        each(s, "b1", {"a": others, "c": 0}, "b", "a")
+                self.mail.received((s, q, after))
+            rest = (slice(None), pl.ds(*self.groups[s][q]))
+
+            def part(at):
+                return self.buf.at[pick({**{named[n]: v for n, v in sel.items()}, axis: at}) + rest]
+
+            for k in (1, 3, 2):
+                self.mail.send((s, q, tag), part(pl.ds(1, 3)), part(0), part(N - k), toward(axis, k))
+
+    def open(self, s):
+        self.each(s, "a", {"b": 0, "c": 0}, "a")
+        self.each(s, "b0", {"a": 0, "c": 0}, "b")
         if s == 0:
-            each(s, "c1", {"a": others, "b": 0}, "c")
-    each(0, "c2", {"a": 0, "b": others}, "c", "b0")
-    each(0, "c3", {"a": others, "b": others}, "c", "b1")
-    each(1, "c0", {"a": 0, "b": 0}, "c")
-    each(1, "c1", {"a": others, "b": 0}, "c")
-    each(1, "c2", {"a": 0, "b": others}, "c", "b0")
-    each(1, "c3", {"a": others, "b": others}, "c", "b1")
+            self.each(0, "c0", {"a": 0, "b": 0}, "c")
+
+    def relay(self):
+        others = pl.ds(1, 3)
+        for s in WAVES:
+            self.each(s, "b1", {"a": others, "c": 0}, "b", "a")
+            if s == 0:
+                self.each(s, "c1", {"a": others, "b": 0}, "c")
+        self.each(0, "c2", {"a": 0, "b": others}, "c", "b0")
+        self.each(0, "c3", {"a": others, "b": others}, "c", "b1")
+        self.each(1, "c0", {"a": 0, "b": 0}, "c")
+        self.each(1, "c1", {"a": others, "b": 0}, "c")
+        self.each(1, "c2", {"a": 0, "b": others}, "c", "b0")
+        self.each(1, "c3", {"a": others, "b": others}, "c", "b1")
 
 
 def gather_end(buf, out, mail, groups, s):
@@ -211,15 +248,15 @@
     return line[32 - keep :]
 
 
-def away(i, j, k):
-    offsets = (i, j, k)
-    return {name: lax.rem(lax.axis_index(name) + offsets[n], N) for n, name in enumerate(AXES)}
-
-
-FAR = sorted(
-    ((i, j, k) for i in range(N) for j in range(N) for k in range(N)),
-    key=lambda at: -sum(min(v, N - v) for v in at),
-)
+def row_factors(C):
+    lane = lax.broadcasted_iota(jnp.int32, (1, N**3 * 4), 1)
+    total = jnp.zeros((1, N**3 * 4), jnp.float32)
+    for i in range(N):
+        for j in range(N):
+            for k in range(N):
+                line = jnp.concatenate([C[i, j, k]] * (N**3 * 4 // 128), axis=1)
+                total = total + jnp.where(lane // 4 == (i * N + j) * N + k, line, 0.0)
+    return total
 
 
 def slot_stats(LT, M, Q, V, IDS, ST, U, mail, columns):
@@ -283,10 +320,7 @@
             if (i * N**2 + j * N + k) * 4 // 128 == t:
                 to = U if at == (0, 0, 0) else ST
                 to[i, j, k] = V[pl.ds(((i * N + j) * N + k) * 4, 4), :]
-        for at in FAR[:-1]:
-            i, j, k = at
-            if (i * N**2 + j * N + k) * 4 // 128 == t:
-                mail.send(0, ST.at[i, j, k], U.at[(N - i) % N, (N - j) % N, (N - k) % N], away(i, j, k))
+        mail.spread(lambda *at: ST.at[at], U, lambda at: (at[0] * N**2 + at[1] * N + at[2]) * 4 // 128 == t)
 
 
 def merged(U, V, Q):
@@ -331,8 +365,8 @@
 def score_kernel(
     h_ref, gf_ref, gl_ref, wg_ref, wu_ref, wd_ref, hw_ref, ids_ref, sid_ref,
     out_ref,
-    HS, G, X, S, R1, R2, R3, T1, T2, F, PB, W, WD, Y, ACT, HB, LT, M, Q, V, IDS, ST, U, A, B,
-    own_s, swap_s, swap_r, g_s, g_r, r_s, r_r, g2_s, g2_r, a_s, a_r, q_s, q_r,
+    HS, G, X, S, R1, R2, R3, T1, T2, PB, W, WD, Y, ACT, HB, LT, M, Q, V, IDS, ST, U, A, B, C, FS,
+    own_s, swap_s, swap_r, g_s, g_r, r_s, r_r, g2_s, g2_r, a_s, a_r, q_s, q_r, c_s, c_r,
 ):
     width = h_ref.shape[-1]
     groups = column_groups(width)
@@ -353,8 +387,11 @@
     mail = Mail(g_s, g_r)
     swap = Mail(swap_s, swap_r)
     for tag, src, dst in (("g", wg_ref, W.at[2]), ("u", wu_ref, W.at[3]), ("d", wd_ref, WD.at[1])):
-        swap.send(tag, src, dst, partner())
-    gather_start(G, mail, groups)
+        swap.send(tag, dst, src, dst, partner())
+    gather = Gather(G, mail, groups)
+    for s in WAVES:
+        gather.open(s)
+    gather.relay()
     order_ids(ids_ref, IDS, Q, V, own)
     for copy in loads[:2]:
         copy.wait()
@@ -366,7 +403,7 @@
         Y[...] = part if s == 0 else Y[...] + part
     loads[2].wait()
     swap.received("d")
-    swap.send("h", hw_ref, HB.at[1], partner())
+    swap.send("h", HB.at[1], hw_ref, HB.at[1], partner())
     own_head = pltpu.make_async_copy(hw_ref, HB.at[0], own_s.at[3])
     own_head.start()
     acts = []
@@ -394,7 +431,8 @@
         down(start, size)
         rest = (slice(None), cols)
         for k in (2, 1, 3):
-            red.send((s, q, 1), S.at[pick({c: k}) + rest], R1.at[(k - 1, slice(None), slice(None)) + rest], toward(c, k))
+            whole = R1.at[:, :, :, :, cols]
+            red.send((s, q, 1), whole, S.at[pick({c: k}) + rest], R1.at[k - 1, :, :, :, cols], toward(c, k))
     for s, q, cols, a, b, c in every:
         red.received((s, q, 1))
 
@@ -413,7 +451,7 @@
         first = min(a, b)
         for k in (2, 1, 3):
             src = T1.at[k, :, :, cols] if b == first else T1.at[:, k, :, cols]
-            red.send((s, q, 2), src, R2.at[k - 1, :, :, cols], toward(b, k))
+            red.send((s, q, 2), R2.at[:, :, :, cols], src, R2.at[k - 1, :, :, cols], toward(b, k))
     for s, q, cols, a, b, c in every:
         red.received((s, q, 2))
         first = min(a, b)
@@ -423,23 +461,35 @@
                 total += R2[k, i, :, cols].astype(jnp.float32)
             T2[i, :, cols] = total.astype(jnp.bfloat16)
         for k in (2, 1, 3):
-            red.send((s, q, 3), T2.at[k, :, cols], R3.at[k - 1, :, cols], toward(a, k))
-    for s, q, cols, a, b, c in every:
-        red.received((s, q, 3))
-        total = T2[0, :, cols].astype(jnp.float32)
-        for k in range(3):
-            total += R3[k, :, cols].astype(jnp.float32)
-        F[:, cols] = total
-
-    residual = (HS[...] + F[...]).astype(jnp.bfloat16)
-    G[0, 0, 0] = rms(residual.astype(jnp.float32), gl_ref[...])
+            red.send((s, q, 3), R3.at[:, :, cols], T2.at[k, :, cols], R3.at[k - 1, :, cols], toward(a, k))
     mail2 = Mail(g2_s, g2_r)
-    gather_start(G, mail2, groups)
+    gather = Gather(G, mail2, groups)
+    squares = jnp.zeros((4, 1), jnp.float32)
+    for s in WAVES:
+        for q in range(3):
+            cols = pl.ds(*groups[s][q])
+            red.received((s, q, 3))
+            total = T2[0, :, cols].astype(jnp.float32)
+            for k in range(3):
+                total += R3[k, :, cols].astype(jnp.float32)
+            residual = (HS[:, cols] + total).astype(jnp.bfloat16).astype(jnp.float32)
+            squares += jnp.sum(residual * residual, axis=-1, keepdims=True)
+            G[0, 0, 0, :, cols] = (residual * gl_ref[:, cols]).astype(jnp.bfloat16)
+        gather.open(s)
+    factor = jnp.broadcast_to(lax.rsqrt(squares / width + EPS), (4, 128))
+    turn = lax.rem(lax.broadcasted_iota(jnp.int32, (4, 128), 1), 4) == lax.broadcasted_iota(jnp.int32, (4, 128), 0)
+    C[0, 0, 0] = jnp.sum(jnp.where(turn, factor, 0.0), axis=0, keepdims=True)
+    gather.relay()
+    scales = Mail(c_s, c_r)
+    scales.spread(lambda *at: C.at[0, 0, 0], C)
     swap.received("h")
     own_head.wait()
     half, tall = LT.shape[0] // 2, 512
     for s in WAVES:
         gather_end(G, X, mail2, groups, s)
+        if s == WAVES[-1]:
+            scales.all_received()
+            FS[...] = row_factors(C)
         for p in range(2):
             if s == 0:
                 LT[pl.ds(p * half + columns // 8 * 8, half - columns // 8 * 8), :] = jnp.full(
@@ -449,24 +499,23 @@
             def logits(at, size):
                 part = by_tokens(lambda cols: HB[p, pl.ds(at, size), cols], X, groups, s)
                 to = pl.ds(p * half + at, size)
-                LT[to, :] = part if s == 0 else LT[to, :] + part
+                LT[to, :] = part if s == 0 else (LT[to, :] + part) * FS[...]
 
             for at in range(0, columns, tall):
                 logits(at, min(tall, columns - at))
 
     stats = Mail(a_s, a_r)
     slot_stats(LT, M, Q, V, IDS, ST, U, stats, columns)
-    stats.received(0)
+    stats.all_received()
     logprob, log_norm, mass = merged(U, V, Q)
 
     A[0] = by_sequence(logprob, sid_ref)
     seq = Mail(q_s, q_r)
-    seq.send(0, A.at[0], A.at[1], partner())
-    seq.received(0)
+    swap.send("s", A.at[1], A.at[0], A.at[1], partner())
+    swap.received("s")
     B[0, 0, 0] = A[0] + A[1]
-    for i, j, k in FAR[:-1]:
-        seq.send(1, B.at[0, 0, 0], B.at[(N - i) % N, (N - j) % N, (N - k) % N], away(i, j, k))
-    seq.received(1)
+    seq.spread(lambda *at: B.at[0, 0, 0], B)
+    seq.all_received()
 
     def joined(values):
         return (values[0] + values[2]) + (values[1] + values[3])
@@ -475,7 +524,7 @@
     for n, value in enumerate((logprob, log_norm, mass, both)):
         out_ref[pl.ds(n, 1), :] = value
     out_ref[4:8, :] = jnp.zeros((4, 128), jnp.float32)
-    for m in (swap, red, mail2, stats, seq):
+    for m in (swap, red, mail2, scales, stats, seq):
         m.all_sent()
 
 
@@ -503,7 +552,6 @@
             pltpu.VMEM((3, 4, width), bf16),
             pltpu.VMEM((N, N, 4, width), bf16),
             pltpu.VMEM((N, 4, width), bf16),
-            pltpu.VMEM((4, width), f32),
             pltpu.VMEM((N * N, N * 4, 1280), bf16),
             pltpu.VMEM((4, hidden, width), bf16),
             pltpu.VMEM((2, hidden, width), bf16),
@@ -518,7 +566,9 @@
             stat, stat,
             pltpu.VMEM((2, 1, 128), f32),
             pltpu.VMEM((N, N, N, 1, 128), f32),
-            dma(4), dma(4), dma(4), dma(126), dma(126), dma(54), dma(54), dma(126), dma(126), dma(63), dma(63), dma(64), dma(64),
+            pltpu.VMEM((N, N, N, 1, 128), f32),
+            pltpu.VMEM((1, rows), f32),
+            dma(4), dma(5), dma(5), dma(42), dma(42), dma(18), dma(18), dma(42), dma(42), dma(3), dma(3), dma(3), dma(3), dma(3), dma(3),
         ],
         compiler_params=pltpu.CompilerParams(collective_id=0, has_side_effects=True, vmem_limit_bytes=67043328),
         name="score",

time: 111 us -> 103 us (0.928)
  Pallas kernels: 109 us -> 101 us
    pallas_call x1, Pallas kernels: 108 us -> 100 us  [score(): pl.pallas_call(score_kernel, out_shape=jax.ShapeDtypeStruct((8, 128), f32...]
where the time goes in v4:
time: 103 us; the launch traced here: 102 us
  Pallas kernels  101 us (98%)
    pallas_call x1, Pallas kernels, score(): pl.pallas_call(score_kernel, out_shape=jax.ShapeDtypeStruct((8, 128), f32...  100 us

profile of v4, /device:TPU:0, one launch (start us, length us, event | category | flops | bytes accessed | tf_op | source)
XLA Modules:
  0.0 102.0 jit_solution(5765911108082994389)
XLA Ops:
  0.6 100.0 %score.1.x_ref = f32[8,128]{1,0:T(8,128)} custom-call(bf16[2,2,7168]{2,1,0:T(2,128)(2,1)} %h_ref.1, f32[1,7168]{1,0:T(1,128)} %bitcast.8, f32[1,7168]{1,0:T(1,128)} %bitcast.9, bf16[144,7168]{1,0:T(8,128)(2,1)} %bitcast.6, bf16[144,7168]{1,0:T(8,128)(2,1)} %bitcast.7, bf16[144,7168]{1,0:T(8,128)(2,1)} %wd_ref.1, bf16[1010,7168]{1,0:T(8,128)(2,1)} %bitcast.5, ...), custom_call_target="tpu_custom_call" | custom-call | tf_op jit(solution)/shard_map/score/pallas_call | solution.py:540
  100.7 1.3 %emit.1 = (f32[2,2]{1,0:T(2,128)}, f32[2,2]{1,0:T(2,128)}, f32[2,2]{1,0:T(2,128)}, f32[2,8]{1,0:T(2,128)}) custom-call(f32[8,128]{1,0:T(8,128)} %score.1.x_ref), custom_call_target="tpu_custom_call" | custom-call | tf_op jit(solution)/shard_map/emit/pallas_call | solution.py:589

commit v5 on v4

--- a/solution.py
+++ b/solution.py
@@ -14,6 +14,7 @@
 NEG = -3.0e38
 MESH = pl.DeviceIdType.MESH
 CORE = "section"
+WAVES = (0, 1, 2)
 AXES = ("x", "z", "y")
 EVERY = (CORE,) + AXES
 ORDERS = ((0, 1, 2), (1, 2, 0), (2, 0, 1))
@@ -27,13 +28,13 @@
 def column_groups(width):
     tiles = width // 128
     cuts = [0, (tiles + 2) // 3, (2 * tiles + 2) // 3, tiles]
-    waves = [[], []]
+    waves = [[] for _ in WAVES]
     for q in range(3):
-        size = cuts[q + 1] - cuts[q]
-        half = (size + 1) // 2 if q < 2 else size // 2 - (size // 2) % 2
-        at = 128 * cuts[q]
-        waves[0].append((at, 128 * half))
-        waves[1].append((at + 128 * half, 128 * (size - half)))
+        tile, size = cuts[q], cuts[q + 1] - cuts[q]
+        for n, wave in enumerate(waves):
+            part = size // len(waves) + (1 if (n - q) % len(waves) < size % len(waves) else 0)
+            wave.append((128 * tile, 128 * part))
+            tile += part
     return waves
 
 
@@ -117,9 +118,6 @@
             self.received(tag)
 
 
-WAVES = (0, 1)
-
-
 class Gather:
     def __init__(self, buf, mail, groups):
         self.buf, self.mail, self.groups = buf, mail, groups
@@ -152,10 +150,11 @@
                 self.each(s, "c1", {"a": others, "b": 0}, "c")
         self.each(0, "c2", {"a": 0, "b": others}, "c", "b0")
         self.each(0, "c3", {"a": others, "b": others}, "c", "b1")
-        self.each(1, "c0", {"a": 0, "b": 0}, "c")
-        self.each(1, "c1", {"a": others, "b": 0}, "c")
-        self.each(1, "c2", {"a": 0, "b": others}, "c", "b0")
-        self.each(1, "c3", {"a": others, "b": others}, "c", "b1")
+        for s in WAVES[1:]:
+            self.each(s, "c0", {"a": 0, "b": 0}, "c")
+            self.each(s, "c1", {"a": others, "b": 0}, "c")
+            self.each(s, "c2", {"a": 0, "b": others}, "c", "b0")
+            self.each(s, "c3", {"a": others, "b": others}, "c", "b1")
 
 
 def gather_end(buf, out, mail, groups, s):
@@ -499,7 +498,8 @@
             def logits(at, size):
                 part = by_tokens(lambda cols: HB[p, pl.ds(at, size), cols], X, groups, s)
                 to = pl.ds(p * half + at, size)
-                LT[to, :] = part if s == 0 else (LT[to, :] + part) * FS[...]
+                total = part if s == 0 else LT[to, :] + part
+                LT[to, :] = total * FS[...] if s == WAVES[-1] else total
 
             for at in range(0, columns, tall):
                 logits(at, min(tall, columns - at))
@@ -568,7 +568,7 @@
             pltpu.VMEM((N, N, N, 1, 128), f32),
             pltpu.VMEM((N, N, N, 1, 128), f32),
             pltpu.VMEM((1, rows), f32),
-            dma(4), dma(5), dma(5), dma(42), dma(42), dma(18), dma(18), dma(42), dma(42), dma(3), dma(3), dma(3), dma(3), dma(3), dma(3),
+            dma(4), dma(5), dma(5), dma(21 * len(WAVES)), dma(21 * len(WAVES)), dma(9 * len(WAVES)), dma(9 * len(WAVES)), dma(21 * len(WAVES)), dma(21 * len(WAVES)), dma(3), dma(3), dma(3), dma(3), dma(3), dma(3),
         ],
         compiler_params=pltpu.CompilerParams(collective_id=0, has_side_effects=True, vmem_limit_bytes=67043328),
         name="score",

time: 103 us -> 100 us (0.971)
  Pallas kernels: 101 us -> 98.2 us
    pallas_call x1, Pallas kernels: 100 us -> 96.9 us  [score(): pl.pallas_call(score_kernel, out_shape=jax.ShapeDtypeStruct((8, 128), f32...]
where the time goes in v5:
time: 100 us; the launch traced here: 98.9 us
  Pallas kernels  98.2 us (98%)
    pallas_call x1, Pallas kernels, score(): pl.pallas_call(score_kernel, out_shape=jax.ShapeDtypeStruct((8, 128), f32...  96.9 us

profile of v5, /device:TPU:0, one launch (start us, length us, event | category | flops | bytes accessed | tf_op | source)
XLA Modules:
  0.0 98.9 jit_solution(18074327951106350278)
XLA Ops:
  0.6 96.9 %score.1.x_ref = f32[8,128]{1,0:T(8,128)} custom-call(bf16[2,2,7168]{2,1,0:T(2,128)(2,1)} %h_ref.1, f32[1,7168]{1,0:T(1,128)} %bitcast.8, f32[1,7168]{1,0:T(1,128)} %bitcast.9, bf16[144,7168]{1,0:T(8,128)(2,1)} %bitcast.6, bf16[144,7168]{1,0:T(8,128)(2,1)} %bitcast.7, bf16[144,7168]{1,0:T(8,128)(2,1)} %wd_ref.1, bf16[1010,7168]{1,0:T(8,128)(2,1)} %bitcast.5, ...), custom_call_target="tpu_custom_call" | custom-call | tf_op jit(solution)/shard_map/score/pallas_call | solution.py:540
  97.5 1.3 %emit.1 = (f32[2,2]{1,0:T(2,128)}, f32[2,2]{1,0:T(2,128)}, f32[2,2]{1,0:T(2,128)}, f32[2,8]{1,0:T(2,128)}) custom-call(f32[8,128]{1,0:T(8,128)} %score.1.x_ref), custom_call_target="tpu_custom_call" | custom-call | tf_op jit(solution)/shard_map/emit/pallas_call | solution.py:589
